TPU v7x, 512 devices: a whole 4x8x8 slice. The times are simulated.
512 devices in a mesh: team: 32 (over x_hi, y, core), rep: 16 (over x_lo, z).
Axes of the slice: x: 4 (x_hi: 2, x_lo: 2; x = x_hi * 2 + x_lo), y: 8, z: 8, core: 2. Of those that a mesh axis runs over, the one named last changes fastest.
Arguments:
- points: bfloat16 [32768, 128], P('team'), may hold values from -3 to 3
Outputs:
- potential: float32 [32768], P('team')
- displacement: float32 [32768, 128], P('team')
All inputs are finite; a program needn't handle non-finite values.
Results may differ from a plain program's by a relative error of at most 0.0097.
The roundings to bfloat16 on the way count: a program that leaves them out, or rounds other values in their place, can miss the bound.
Values may be sent and summed in bfloat16 or wider, within the bound.
A program may use at most 64 MiB of HBM per device.

v0:
```python
import jax
import jax.numpy as jnp
from jax import lax
from jax.sharding import PartitionSpec as P


def shifted(block, axis, distance):
    devices = range(lax.axis_size(axis))
    route = [((i - distance) % len(devices), i) for i in devices]
    return lax.ppermute(block, axis, route)


def square_norms(block_points):
    return jnp.sum(jnp.square(block_points.astype(jnp.float32)), axis=1)


def digit_set(offset, bit_index):
    return jnp.right_shift(offset, bit_index) % 2 == 1


def deliver_partner(block_points, offset):
    digits = lax.axis_size("rep").bit_length()
    current = block_points
    for bit_index in range(digits):
        arrived = shifted(current, "team", -(1 << bit_index))
        current = jnp.where(digit_set(offset, bit_index), arrived, current)
    return current


def potential_partner(pot_one, offset):
    digits = lax.axis_size("rep").bit_length()
    current = pot_one
    for bit_index in range(digits):
        arrived = shifted(current, "team", -(1 << bit_index))
        current = jnp.where(digit_set(offset, bit_index), arrived, current)
    return current


def return_sums(col_total, offset):
    digits = lax.axis_size("rep").bit_length()
    current = col_total
    for bit_index in range(digits):
        arrived = shifted(current, "team", 1 << bit_index)
        current = jnp.where(digit_set(offset, bit_index), arrived, current)
    return current


def return_both(col_total, col_numer, offset):
    digits = lax.axis_size("rep").bit_length()
    current_total = col_total
    current_numer = col_numer
    for bit_index in range(digits):
        arrived = shifted((current_total, current_numer), "team", 1 << bit_index)
        chosen = digit_set(offset, bit_index)
        current_total = jnp.where(chosen, arrived[0], current_total)
        current_numer = jnp.where(chosen, arrived[1], current_numer)
    return (current_total, current_numer)


def tile_sums(row_side, col_side, inv_eps, want_cols, with_num):
    rows_x, rows_sq, rows_pot = row_side
    cols_x, cols_sq, cols_pot = col_side
    block_rows = rows_x.shape[0]
    numer_width = rows_x.shape[1] if with_num else 0
    col_count = block_rows if want_cols else 0
    row_block = min(block_rows, 512)
    col_block = min(block_rows, 256)
    rows_scale = jnp.exp(rows_pot * inv_eps)
    cols_scale = jnp.exp(cols_pot * inv_eps)
    initial = (
        jnp.zeros((block_rows,), jnp.float32),
        jnp.zeros((block_rows, numer_width), jnp.float32),
        jnp.zeros((col_count,), jnp.float32),
        jnp.zeros((col_count, numer_width), jnp.float32),
    )

    def row_step(row_index, carried):
        row_total, row_numer, col_total, col_numer = carried
        row_start = row_index * row_block
        part_x = lax.dynamic_slice_in_dim(rows_x, row_start, row_block, 0)
        part_sq = lax.dynamic_slice_in_dim(rows_sq, row_start, row_block, 0)
        part_scale = lax.dynamic_slice_in_dim(rows_scale, row_start, row_block, 0)

        def col_step(col_index, inner_carried):
            block_total, block_numer, col_acc, col_num_acc = inner_carried
            col_start = col_index * col_block
            other_x = lax.dynamic_slice_in_dim(cols_x, col_start, col_block, 0)
            other_sq = lax.dynamic_slice_in_dim(cols_sq, col_start, col_block, 0)
            other_scale = lax.dynamic_slice_in_dim(cols_scale, col_start, col_block, 0)
            products = lax.dot_general(
                part_x, other_x, (((1,), (1,)), ((), ())), preferred_element_type=jnp.float32
            )
            kernel = jnp.exp(
                (products - 0.5 * part_sq[:, None] - 0.5 * other_sq[None, :]) * inv_eps
            )
            row_weight = kernel * other_scale[None, :]
            block_total = block_total + jnp.sum(row_weight, axis=1)
            if with_num:
                block_numer = block_numer + jnp.dot(
                    row_weight.astype(jnp.bfloat16), other_x, preferred_element_type=jnp.float32
                )
            if want_cols:
                col_weight = kernel * part_scale[:, None]
                col_piece = lax.dynamic_slice_in_dim(col_acc, col_start, col_block, 0) + jnp.sum(
                    col_weight, axis=0
                )
                col_acc = lax.dynamic_update_slice_in_dim(col_acc, col_piece, col_start, 0)
                if with_num:
                    col_added = lax.dot_general(
                        col_weight.astype(jnp.bfloat16),
                        part_x,
                        (((0,), (0,)), ((), ())),
                        preferred_element_type=jnp.float32,
                    )
                    num_piece = (
                        lax.dynamic_slice_in_dim(col_num_acc, col_start, col_block, 0) + col_added
                    )
                    col_num_acc = lax.dynamic_update_slice_in_dim(
                        col_num_acc, num_piece, col_start, 0
                    )
            return (block_total, block_numer, col_acc, col_num_acc)

        start_inner = (
            jnp.zeros((row_block,), jnp.float32),
            jnp.zeros((row_block, numer_width), jnp.float32),
            col_total,
            col_numer,
        )
        block_total, block_numer, col_total, col_numer = lax.fori_loop(
            0, block_rows // col_block, col_step, start_inner
        )
        row_total = lax.dynamic_update_slice_in_dim(row_total, block_total, row_start, 0)
        row_numer = lax.dynamic_update_slice_in_dim(row_numer, block_numer, row_start, 0)
        return (row_total, row_numer, col_total, col_numer)

    return lax.fori_loop(0, block_rows // row_block, row_step, initial)


def paired_sums(own_side, partner_side, offset, replica, kept_share, inv_eps, with_num):
    row_total, row_numer, col_total, col_numer = tile_sums(
        own_side, partner_side, inv_eps, True, with_num
    )

    def diagonal(unused):
        diag_values = tile_sums(own_side, own_side, inv_eps, False, with_num)
        return (diag_values[0], diag_values[1])

    def nothing(unused):
        return (jnp.zeros_like(row_total), jnp.zeros_like(row_numer))

    diag_total, diag_numer = lax.cond(replica == 0, diagonal, nothing, 0)
    if with_num:
        back_total, back_numer = return_both(col_total * kept_share, col_numer * kept_share, offset)
        return (
            row_total * kept_share + diag_total + back_total,
            row_numer * kept_share + diag_numer + back_numer,
        )
    back_total = return_sums(col_total * kept_share, offset)
    return (row_total * kept_share + diag_total + back_total, row_numer)


def neighbour_potentials(pot_one, offset, replica):
    partner_pot = potential_partner(pot_one, offset)
    mirror_pot = pot_one
    mirror_pot = jnp.where(replica == 0, pot_one, mirror_pot)
    return (partner_pot, mirror_pot)


def shards(points):
    block_rows = points.shape[0]
    replicas = lax.axis_size("rep")
    team_count = lax.axis_size("team")
    replica = lax.axis_index("rep")
    team_index = lax.axis_index("team")
    offset = jnp.where(replica == 0, replicas, replica)
    own_sq = square_norms(points)
    log_count = jnp.log(jnp.float32(block_rows * team_count))
    zero_pot = jnp.zeros((block_rows,), jnp.float32)
    partner_x = deliver_partner(points, offset)
    partner_sq = square_norms(partner_x)
    kept_share = jnp.where((replica != 0) | (team_index < replicas), 1.0, 0.0).astype(jnp.float32)
    first_local, unused_numer = paired_sums(
        (points, own_sq, zero_pot),
        (partner_x, partner_sq, zero_pot),
        offset,
        replica,
        kept_share,
        0.25,
        False,
    )
    first_sum = lax.psum(first_local, "rep")
    pot_one = 0.5 * (zero_pot - 4.0 * (jnp.log(first_sum) - log_count))
    partner_pot, mirror_pot = neighbour_potentials(pot_one, offset, replica)
    second_local, numer_local = paired_sums(
        (points, own_sq, pot_one),
        (partner_x, partner_sq, partner_pot),
        offset,
        replica,
        kept_share,
        0.5,
        True,
    )
    second, numerator = lax.psum((second_local, numer_local), "rep")
    potential = 0.5 * (pot_one - 2.0 * (jnp.log(second) - log_count))
    displacement = points.astype(jnp.float32) - numerator / second[:, None]
    return (potential, displacement)


def solution(mesh):
    return jax.shard_map(
        shards,
        mesh=mesh,
        in_specs=(P("team", None),),
        out_specs=(P("team"), P("team", None)),
        check_vma=False,
    )
```

profile of v0, /device:TPU:56, one launch (start us, length us, event | category | flops | bytes accessed | tf_op | source)
XLA Modules:
  0.0 475.6 jit_solution(9570896007288709853)
XLA Ops:
  7.2 2.7 collective-permute-start
  9.9 4.2 collective-permute-done
  15.1 3.3 collective-permute-start.1
  18.4 8.6 %collective-permute-done.1 = bf16[1024,128]{1,0:T(8,128)(2,1)S(1)} collective-permute-done((bf16[1024,128]{1,0:T(8,128)(2,1)S(1)}, bf16[1024,128]{1,0:T(8,128)(2,1)S(1)}, u32[]{:S(2)}, u32[]{:S(2)}) %collective-permute-start.1) | collective-permute-done | bytes 262176 | tf_op jit(solution)/shard_map/ppermute | solution.py:10
  27.0 3.1 collective-permute-start.2
  30.1 16.3 %collective-permute-done.2 = bf16[1024,128]{1,0:T(8,128)(2,1)S(1)} collective-permute-done((bf16[1024,128]{1,0:T(8,128)(2,1)S(1)}, bf16[1024,128]{1,0:T(8,128)(2,1)S(1)}, u32[]{:S(2)}, u32[]{:S(2)}) %collective-permute-start.2) | collective-permute-done | bytes 262176 | tf_op jit(solution)/shard_map/ppermute | solution.py:10
  46.5 1.9 collective-permute-start.3
  48.4 17.3 %collective-permute-done.3 = bf16[1024,128]{1,0:T(8,128)(2,1)S(1)} collective-permute-done((bf16[1024,128]{1,0:T(8,128)(2,1)S(1)}, bf16[1024,128]{1,0:T(8,128)(2,1)S(1)}, u32[]{:S(2)}, u32[]{:S(2)}) %collective-permute-start.3) | collective-permute-done | bytes 262176 | tf_op jit(solution)/shard_map/ppermute | solution.py:10
  65.7 1.9 collective-permute-start.4
  67.9 9.5 %collective-permute-done.4 = bf16[1024,128]{1,0:T(8,128)(2,1)S(1)} collective-permute-done((bf16[1024,128]{1,0:T(8,128)(2,1)S(1)}, bf16[1024,128]{1,0:T(8,128)(2,1)S(1)}, u32[]{:S(2)}, u32[]{:S(2)}) %collective-permute-start.4) | collective-permute-done | bytes 262176 | tf_op jit(solution)/shard_map/ppermute | solution.py:10
  77.6 5.8 %while.193 = (s32[]{:T(128)}, f32[1024]{0:T(1024)S(1)}, f32[1024]{0:T(1024)S(1)}, bf16[1024,128]{1,0:T(8,128)(2,1)S(1)}, f32[1024]{0:T(1024)S(1)}, /*index=5*/bf...) while((s32[]{:T(128)}, f32[1024]{0:T(1024)S(1)}, ...), condition=%wide.region_7.8_spmd, body=%wide.region_2.7_spmd.sunk | while | flops 34211080 | bytes 488936 | solution.py:136
  77.8 2.6 while.196
  80.6 2.6 while.196
  83.4 1.9 collective-permute-start.5
  85.3 3.0 collective-permute-done.5
  88.3 4.6 collective-permute-start.6
  94.2 3.6 collective-permute-start.7
  97.9 2.8 collective-permute-done.7
  100.6 5.6 %collective-permute-start.8 = (f32[1024]{0:T(1024)S(1)}, f32[1024]{0:T(1024)S(1)}, u32[]{:S(2)}, u32[]{:S(2)}) collective-permute-start(f32[1024]{0:T(1024)S(1)} %broadcast_select_fusion.17), channel_id=1, source_target_pairs={{384,0},{400,16},{416,32},{432,48},{448,64},{464,80},{480,96},{496... | collective-permute-start | bytes 12296 | tf_op jit(solution)/shard_map/ppermute | solution.py:10
  106.2 3.8 collective-permute-done.8
  110.0 4.3 collective-permute-start.9
  114.3 6.8 %conditional.2 = (f32[1024]{0:T(1024)}) conditional(s32[]{:T(128)} %convert_element_type.34, () %tuple.143, (bf16[1024,128]{1,0:T(8,128)(2,1)S(1)}, f32[1024]{0:T(1024)S(1)}) %tuple.293), branch_computations={%region_8.9_spmd, %region_9.15_spmd} | conditional | flops 34080008 | bytes 489008 | solution.py:151
  114.9 6.2 %while.187 = (s32[]{:T(128)}, f32[1024]{0:T(1024)}, bf16[1024,128]{1,0:T(8,128)(2,1)S(1)}, f32[1024]{0:T(1024)S(1)}, s32[]{:T(128)}, /*index=5*/s32[]{:T(128)}, ...) while((s32[]{:T(128)}, f32[1024]{0:T(1024)}, ...), condition=%wide.region_14.14_spmd, body=%wide.region_10.13_spmd.sunk | while | flops 34080008 | bytes 484796 | solution.py:136
  115.0 1.6 while.199
  118.1 1.6 while.199
  121.8 35.3 %psum.21 = f32[1024]{0:T(1024)S(1)} all-reduce(f32[1024]{0:T(1024)S(1)} %select_add_fusion.6), channel_id=1, replica_groups=mesh['team'=32,'rep'=16] {'rep'}, use_global_device_ids=true, to_apply=%region_15.16 | all-reduce | flops 1024 | bytes 8192 | tf_op jit(solution)/shard_map/psum | solution.py:191
  157.1 1.9 collective-permute-start.10
  160.3 5.9 %collective-permute-start.11 = (f32[1024]{0:T(1024)S(1)}, f32[1024]{0:T(1024)S(1)}, u32[]{:S(2)}, u32[]{:S(2)}) collective-permute-start(f32[1024]{0:T(1024)S(1)} %get-tuple-element.1415), channel_id=1, source_target_pairs={{32,0},{48,16},{64,32},{80,48},{96,64},{112,80},{128,96},{144,112}... | collective-permute-start | bytes 12296 | tf_op jit(solution)/shard_map/ppermute | solution.py:10
  166.2 9.9 %collective-permute-done.11 = f32[1024]{0:T(1024)S(1)} collective-permute-done((f32[1024]{0:T(1024)S(1)}, f32[1024]{0:T(1024)S(1)}, u32[]{:S(2)}, u32[]{:S(2)}) %collective-permute-start.11) | collective-permute-done | bytes 4128 | tf_op jit(solution)/shard_map/ppermute | solution.py:10
  176.1 1.9 collective-permute-start.12
  178.0 8.1 %collective-permute-done.12 = f32[1024]{0:T(1024)S(1)} collective-permute-done((f32[1024]{0:T(1024)S(1)}, f32[1024]{0:T(1024)S(1)}, u32[]{:S(2)}, u32[]{:S(2)}) %collective-permute-start.12) | collective-permute-done | bytes 4128 | tf_op jit(solution)/shard_map/ppermute | solution.py:10
  186.1 1.9 collective-permute-start.13
  188.0 9.9 %collective-permute-done.13 = f32[1024]{0:T(1024)S(1)} collective-permute-done((f32[1024]{0:T(1024)S(1)}, f32[1024]{0:T(1024)S(1)}, u32[]{:S(2)}, u32[]{:S(2)}) %collective-permute-start.13) | collective-permute-done | bytes 4128 | tf_op jit(solution)/shard_map/ppermute | solution.py:10
  197.9 3.5 collective-permute-start.14
  201.5 3.4 collective-permute-done.14
  205.0 12.1 %while.195 = (s32[]{:T(128)}, f32[1024]{0:T(1024)S(1)}, f32[1024,128]{1,0:T(8,128)S(1)}, f32[1024]{0:T(1024)S(1)}, f32[1024,128]{1,0:T(8,128)S(1)}, /*index=5*/b...) while((s32[]{:T(128)}, f32[1024]{0:T(1024)S(1)}, ...), condition=%wide.region_21.22_spmd, body=%wide.region_16.21_spmd.sunk | while | flops 102270216 | bytes 3581533 | solution.py:136
  205.3 5.5 %while.197 = (s32[]{:T(128)}, f32[512]{0:T(512)S(1)}, f32[512,128]{1,0:T(8,128)S(1)}, f32[1024]{0:T(1024)S(1)}, f32[1024,128]{1,0:T(8,128)S(1)}, /*index=5*/bf16...) while((s32[]{:T(128)}, f32[512]{0:T(512)S(1)}, ...), condition=%wide.region_20.20_spmd.clone, body=%wide.region_17.19_spmd.clone.sunk | while | flops 102270208 | bytes 2782438 | solution.py:129
  211.3 5.5 %while.197 = (s32[]{:T(128)}, f32[512]{0:T(512)S(1)}, f32[512,128]{1,0:T(8,128)S(1)}, f32[1024]{0:T(1024)S(1)}, f32[1024,128]{1,0:T(8,128)S(1)}, /*index=5*/bf16...) while((s32[]{:T(128)}, f32[512]{0:T(512)S(1)}, ...), condition=%wide.region_20.20_spmd.clone, body=%wide.region_17.19_spmd.clone.sunk | while | flops 102270208 | bytes 2782438 | solution.py:129
  217.2 3.0 collective-permute-start.20
  220.2 7.5 %collective-permute-done.20 = f32[1024,128]{1,0:T(8,128)S(1)} collective-permute-done((f32[1024,128]{1,0:T(8,128)S(1)}, f32[1024,128]{1,0:T(8,128)S(1)}, u32[]{:S(2)}, u32[]{:S(2)}) %collective-permute-start.20) | collective-permute-done | bytes 524320 | tf_op jit(solution)/shard_map/ppermute | solution.py:10
  227.8 6.5 %collective-permute-start.21 = (f32[1024,128]{1,0:T(8,128)S(1)}, f32[1024,128]{1,0:T(8,128)S(1)}, u32[]{:S(2)}, u32[]{:S(2)}) collective-permute-start(f32[1024,128]{1,0:T(8,128)S(1)} %broadcast_select_fusion), channel_id=1, source_target_pairs={{480,0},{496,16},{0,32},{16,48},{32,64},{48,80},{64,96},{80,112},{... | collective-permute-start | bytes 1572872 | tf_op jit(solution)/shard_map/ppermute | solution.py:10
  234.3 7.8 %collective-permute-done.21 = f32[1024,128]{1,0:T(8,128)S(1)} collective-permute-done((f32[1024,128]{1,0:T(8,128)S(1)}, f32[1024,128]{1,0:T(8,128)S(1)}, u32[]{:S(2)}, u32[]{:S(2)}) %collective-permute-start.21) | collective-permute-done | bytes 524320 | tf_op jit(solution)/shard_map/ppermute | solution.py:10
  242.2 2.7 collective-permute-start.22
  244.9 21.0 %collective-permute-done.22 = f32[1024,128]{1,0:T(8,128)S(1)} collective-permute-done((f32[1024,128]{1,0:T(8,128)S(1)}, f32[1024,128]{1,0:T(8,128)S(1)}, u32[]{:S(2)}, u32[]{:S(2)}) %collective-permute-start.22) | collective-permute-done | bytes 524320 | tf_op jit(solution)/shard_map/ppermute | solution.py:10
  265.9 4.3 collective-permute-start.23
  270.3 1.9 collective-permute-start.15
  272.2 13.0 %collective-permute-done.23 = f32[1024,128]{1,0:T(8,128)S(1)} collective-permute-done((f32[1024,128]{1,0:T(8,128)S(1)}, f32[1024,128]{1,0:T(8,128)S(1)}, u32[]{:S(2)}, u32[]{:S(2)}) %collective-permute-start.23) | collective-permute-done | bytes 524320 | tf_op jit(solution)/shard_map/ppermute | solution.py:10
  285.2 3.7 collective-permute-start.24
  288.9 3.4 collective-permute-done.15
  292.3 9.6 %collective-permute-start.16 = (f32[1024]{0:T(1024)S(1)}, f32[1024]{0:T(1024)S(1)}, u32[]{:S(2)}, u32[]{:S(2)}) collective-permute-start(f32[1024]{0:T(1024)S(1)} %broadcast_select_fusion.9), channel_id=1, source_target_pairs={{480,0},{496,16},{0,32},{16,48},{32,64},{48,80},{64,96},{80,112},{... | collective-permute-start | bytes 12296 | tf_op jit(solution)/shard_map/ppermute | solution.py:10
  301.9 3.1 collective-permute-done.16
  305.1 7.0 %collective-permute-start.17 = (f32[1024]{0:T(1024)S(1)}, f32[1024]{0:T(1024)S(1)}, u32[]{:S(2)}, u32[]{:S(2)}) collective-permute-start(f32[1024]{0:T(1024)S(1)} %broadcast_select_fusion.12), channel_id=1, source_target_pairs={{448,0},{464,16},{480,32},{496,48},{0,64},{16,80},{32,96},{48,112}... | collective-permute-start | bytes 12296 | tf_op jit(solution)/shard_map/ppermute | solution.py:10
  312.0 12.5 %conditional.3 = (f32[1024]{0:T(1024)}, f32[1024,128]{1,0:T(8,128)}) conditional(s32[]{:T(128)} %convert_element_type.34, () %tuple.146, (f32[1024]{0:T(1024)S(1)}, bf16[1024,128]{1,0:T(8,128)(2,1)S(1)}, f32[1024]{0:T(1024)S(1)}) %tuple.295), branch_computations={%region_22.23_spmd, %region_23.29_spmd} | conditional | flops 68028680 | bytes 2663049 | solution.py:151
  313.5 11.0 %while.191 = (s32[]{:T(128)}, f32[1024]{0:T(1024)}, f32[1024,128]{1,0:T(8,128)}, bf16[1024,128]{1,0:T(8,128)(2,1)S(1)}, f32[1024]{0:T(1024)S(1)}, /*index=5*/f32...) while((s32[]{:T(128)}, f32[1024]{0:T(1024)}, ...), condition=%wide.region_28.28_spmd, body=%wide.region_24.27_spmd.sunk | while | flops 68027656 | bytes 2126329 | solution.py:136
  313.6 3.3 while.198
  319.1 3.3 while.198
  324.5 4.1 collective-permute-start.18
  328.6 2.0 select_add_fusion.4
  330.7 3.3 collective-permute-done.18
  333.9 3.6 collective-permute-start.19
  337.5 3.4 collective-permute-done.19
  341.6 30.6 %psum.22 = f32[1024]{0:T(1024)S(1)} all-reduce(f32[1024]{0:T(1024)S(1)} %select_add_fusion.5), channel_id=1, replica_groups=mesh['team'=32,'rep'=16] {'rep'}, use_global_device_ids=true, to_apply=%region_29.30 | all-reduce | flops 1024 | bytes 8192 | tf_op jit(solution)/shard_map/psum | solution.py:203
  372.9 93.9 %all-reduce.2.cloned.1.call-done = f32[1024,128]{1,0:T(8,128)} async-done(((f32[1024,128]{1,0:T(8,128)}), f32[1024,128]{1,0:T(8,128)}) %all-reduce.2.cloned.1.call-update) | async-done | bytes 524304 | tf_op jit(solution)/shard_map/psum | solution.py:203
  466.7 2.0 convert_subtract_fusion
  (275 shorter events, 42.6 us)
Async XLA Ops:
  7.2 459.5 %all-reduce.2.cloned.1.call-start = ((), (), s32[]{:S(2)}) async-start(), calls=%async_computation | async-start | bytes 1048576 | tf_op jit(solution)/shard_map/psum | solution.py:203
  7.2 6.9 %collective-permute-start = (bf16[1024,128]{1,0:T(8,128)(2,1)}, bf16[1024,128]{1,0:T(8,128)(2,1)S(1)}, u32[]{:S(2)}, u32[]{:S(2)}) collective-permute-start(bf16[1024,128]{1,0:T(8,128)(2,1)} %param.21), channel_id=1, source_target_pairs={{16,0},{32,16},{48,32},{64,48},{80,64},{96,80},{112,96},{128,112},... | collective-permute-start | bytes 786440 | tf_op jit(solution)/shard_map/ppermute | solution.py:10
  15.1 11.9 %collective-permute-start.1 = (bf16[1024,128]{1,0:T(8,128)(2,1)S(1)}, bf16[1024,128]{1,0:T(8,128)(2,1)S(1)}, u32[]{:S(2)}, u32[]{:S(2)}) collective-permute-start(bf16[1024,128]{1,0:T(8,128)(2,1)S(1)} %broadcast_select_fusion.1), channel_id=1, source_target_pairs={{32,0},{48,16},{64,32},{80,48},{96,64},{112,80},{128,96},{144,112}... | collective-permute-start | bytes 786440 | tf_op jit(solution)/shard_map/ppermute | solution.py:10
  27.0 19.4 %collective-permute-start.2 = (bf16[1024,128]{1,0:T(8,128)(2,1)S(1)}, bf16[1024,128]{1,0:T(8,128)(2,1)S(1)}, u32[]{:S(2)}, u32[]{:S(2)}) collective-permute-start(bf16[1024,128]{1,0:T(8,128)(2,1)S(1)} %broadcast_select_fusion.3), channel_id=1, source_target_pairs={{64,0},{80,16},{96,32},{112,48},{128,64},{144,80},{160,96},{176,11... | collective-permute-start | bytes 786440 | tf_op jit(solution)/shard_map/ppermute | solution.py:10
  46.5 19.2 %collective-permute-start.3 = (bf16[1024,128]{1,0:T(8,128)(2,1)S(1)}, bf16[1024,128]{1,0:T(8,128)(2,1)S(1)}, u32[]{:S(2)}, u32[]{:S(2)}) collective-permute-start(bf16[1024,128]{1,0:T(8,128)(2,1)S(1)} %broadcast_select_fusion.5), channel_id=1, source_target_pairs={{128,0},{144,16},{160,32},{176,48},{192,64},{208,80},{224,96},{240... | collective-permute-start | bytes 786440 | tf_op jit(solution)/shard_map/ppermute | solution.py:10
  48.4 19.3 %copy-start = (bf16[1024,128]{1,0:T(8,128)(2,1)S(1)}, bf16[1024,128]{1,0:T(8,128)(2,1)}, u32[]{:S(2)}) copy-start(bf16[1024,128]{1,0:T(8,128)(2,1)} %param.21) | copy-start | bytes 786436
  65.7 11.7 %collective-permute-start.4 = (bf16[1024,128]{1,0:T(8,128)(2,1)S(1)}, bf16[1024,128]{1,0:T(8,128)(2,1)S(1)}, u32[]{:S(2)}, u32[]{:S(2)}) collective-permute-start(bf16[1024,128]{1,0:T(8,128)(2,1)S(1)} %broadcast_select_fusion.7), channel_id=1, source_target_pairs={{256,0},{272,16},{288,32},{304,48},{320,64},{336,80},{352,96},{368... | collective-permute-start | bytes 786440 | tf_op jit(solution)/shard_map/ppermute | solution.py:10
  83.4 4.9 %collective-permute-start.5 = (f32[1024]{0:T(1024)S(1)}, f32[1024]{0:T(1024)S(1)}, u32[]{:S(2)}, u32[]{:S(2)}) collective-permute-start(f32[1024]{0:T(1024)S(1)} %broadcast_multiply_fusion.6), channel_id=1, source_target_pairs={{496,0},{0,16},{16,32},{32,48},{48,64},{64,80},{80,96},{96,112},{1... | collective-permute-start | bytes 12296 | tf_op jit(solution)/shard_map/ppermute | solution.py:10
  88.3 5.9 %collective-permute-start.6 = (f32[1024]{0:T(1024)S(1)}, f32[1024]{0:T(1024)S(1)}, u32[]{:S(2)}, u32[]{:S(2)}) collective-permute-start(f32[1024]{0:T(1024)S(1)} %broadcast_select_fusion.11), channel_id=1, source_target_pairs={{480,0},{496,16},{0,32},{16,48},{32,64},{48,80},{64,96},{80,112},{... | collective-permute-start | bytes 12296 | tf_op jit(solution)/shard_map/ppermute | solution.py:10
  94.2 6.4 %collective-permute-start.7 = (f32[1024]{0:T(1024)S(1)}, f32[1024]{0:T(1024)S(1)}, u32[]{:S(2)}, u32[]{:S(2)}) collective-permute-start(f32[1024]{0:T(1024)S(1)} %broadcast_select_fusion.14), channel_id=1, source_target_pairs={{448,0},{464,16},{480,32},{496,48},{0,64},{16,80},{32,96},{48,112}... | collective-permute-start | bytes 12296 | tf_op jit(solution)/shard_map/ppermute | solution.py:10
  100.6 9.4 %collective-permute-start.8 = (f32[1024]{0:T(1024)S(1)}, f32[1024]{0:T(1024)S(1)}, u32[]{:S(2)}, u32[]{:S(2)}) collective-permute-start(f32[1024]{0:T(1024)S(1)} %broadcast_select_fusion.17), channel_id=1, source_target_pairs={{384,0},{400,16},{416,32},{432,48},{448,64},{464,80},{480,96},{496... | collective-permute-start | bytes 12296 | tf_op jit(solution)/shard_map/ppermute | solution.py:10
  110.0 11.1 %collective-permute-start.9 = (f32[1024]{0:T(1024)S(1)}, f32[1024]{0:T(1024)S(1)}, u32[]{:S(2)}, u32[]{:S(2)}) collective-permute-start(f32[1024]{0:T(1024)S(1)} %broadcast_select_fusion.20), channel_id=1, source_target_pairs={{256,0},{272,16},{288,32},{304,48},{320,64},{336,80},{352,96},{368... | collective-permute-start | bytes 12296 | tf_op jit(solution)/shard_map/ppermute | solution.py:10
  157.1 3.2 collective-permute-start.10
  160.3 15.8 %collective-permute-start.11 = (f32[1024]{0:T(1024)S(1)}, f32[1024]{0:T(1024)S(1)}, u32[]{:S(2)}, u32[]{:S(2)}) collective-permute-start(f32[1024]{0:T(1024)S(1)} %get-tuple-element.1415), channel_id=1, source_target_pairs={{32,0},{48,16},{64,32},{80,48},{96,64},{112,80},{128,96},{144,112}... | collective-permute-start | bytes 12296 | tf_op jit(solution)/shard_map/ppermute | solution.py:10
  176.1 10.0 %collective-permute-start.12 = (f32[1024]{0:T(1024)S(1)}, f32[1024]{0:T(1024)S(1)}, u32[]{:S(2)}, u32[]{:S(2)}) collective-permute-start(f32[1024]{0:T(1024)S(1)} %broadcast_select_fusion.13), channel_id=1, source_target_pairs={{64,0},{80,16},{96,32},{112,48},{128,64},{144,80},{160,96},{176,11... | collective-permute-start | bytes 12296 | tf_op jit(solution)/shard_map/ppermute | solution.py:10
  186.1 11.8 %collective-permute-start.13 = (f32[1024]{0:T(1024)S(1)}, f32[1024]{0:T(1024)S(1)}, u32[]{:S(2)}, u32[]{:S(2)}) collective-permute-start(f32[1024]{0:T(1024)S(1)} %broadcast_select_fusion.16), channel_id=1, source_target_pairs={{128,0},{144,16},{160,32},{176,48},{192,64},{208,80},{224,96},{240... | collective-permute-start | bytes 12296 | tf_op jit(solution)/shard_map/ppermute | solution.py:10
  197.9 7.0 %collective-permute-start.14 = (f32[1024]{0:T(1024)S(1)}, f32[1024]{0:T(1024)S(1)}, u32[]{:S(2)}, u32[]{:S(2)}) collective-permute-start(f32[1024]{0:T(1024)S(1)} %broadcast_select_fusion.19), channel_id=1, source_target_pairs={{256,0},{272,16},{288,32},{304,48},{320,64},{336,80},{352,96},{368... | collective-permute-start | bytes 12296 | tf_op jit(solution)/shard_map/ppermute | solution.py:10
  217.2 10.5 %collective-permute-start.20 = (f32[1024,128]{1,0:T(8,128)S(1)}, f32[1024,128]{1,0:T(8,128)S(1)}, u32[]{:S(2)}, u32[]{:S(2)}) collective-permute-start(f32[1024,128]{1,0:T(8,128)S(1)} %broadcast_multiply_fusion.4), channel_id=1, source_target_pairs={{496,0},{0,16},{16,32},{32,48},{48,64},{64,80},{80,96},{96,112},{1... | collective-permute-start | bytes 1572872 | tf_op jit(solution)/shard_map/ppermute | solution.py:10
  227.8 14.4 %collective-permute-start.21 = (f32[1024,128]{1,0:T(8,128)S(1)}, f32[1024,128]{1,0:T(8,128)S(1)}, u32[]{:S(2)}, u32[]{:S(2)}) collective-permute-start(f32[1024,128]{1,0:T(8,128)S(1)} %broadcast_select_fusion), channel_id=1, source_target_pairs={{480,0},{496,16},{0,32},{16,48},{32,64},{48,80},{64,96},{80,112},{... | collective-permute-start | bytes 1572872 | tf_op jit(solution)/shard_map/ppermute | solution.py:10
  242.2 23.7 %collective-permute-start.22 = (f32[1024,128]{1,0:T(8,128)S(1)}, f32[1024,128]{1,0:T(8,128)S(1)}, u32[]{:S(2)}, u32[]{:S(2)}) collective-permute-start(f32[1024,128]{1,0:T(8,128)S(1)} %broadcast_select_fusion.2), channel_id=1, source_target_pairs={{448,0},{464,16},{480,32},{496,48},{0,64},{16,80},{32,96},{48,112}... | collective-permute-start | bytes 1572872 | tf_op jit(solution)/shard_map/ppermute | solution.py:10
  265.9 19.3 %collective-permute-start.23 = (f32[1024,128]{1,0:T(8,128)S(1)}, f32[1024,128]{1,0:T(8,128)S(1)}, u32[]{:S(2)}, u32[]{:S(2)}) collective-permute-start(f32[1024,128]{1,0:T(8,128)S(1)} %broadcast_select_fusion.4), channel_id=1, source_target_pairs={{384,0},{400,16},{416,32},{432,48},{448,64},{464,80},{480,96},{496... | collective-permute-start | bytes 1572872 | tf_op jit(solution)/shard_map/ppermute | solution.py:10
  270.3 22.1 %collective-permute-start.15 = (f32[1024]{0:T(1024)S(1)}, f32[1024]{0:T(1024)S(1)}, u32[]{:S(2)}, u32[]{:S(2)}) collective-permute-start(f32[1024]{0:T(1024)S(1)} %broadcast_multiply_fusion.5), channel_id=1, source_target_pairs={{496,0},{0,16},{16,32},{32,48},{48,64},{64,80},{80,96},{96,112},{1... | collective-permute-start | bytes 12296 | tf_op jit(solution)/shard_map/ppermute | solution.py:10
  285.2 43.4 %collective-permute-start.24 = (f32[1024,128]{1,0:T(8,128)S(1)}, f32[1024,128]{1,0:T(8,128)S(1)}, u32[]{:S(2)}, u32[]{:S(2)}) collective-permute-start(f32[1024,128]{1,0:T(8,128)S(1)} %broadcast_select_fusion.6), channel_id=1, source_target_pairs={{256,0},{272,16},{288,32},{304,48},{320,64},{336,80},{352,96},{368... | collective-permute-start | bytes 1572872 | tf_op jit(solution)/shard_map/ppermute | solution.py:10
  292.3 12.7 %collective-permute-start.16 = (f32[1024]{0:T(1024)S(1)}, f32[1024]{0:T(1024)S(1)}, u32[]{:S(2)}, u32[]{:S(2)}) collective-permute-start(f32[1024]{0:T(1024)S(1)} %broadcast_select_fusion.9), channel_id=1, source_target_pairs={{480,0},{496,16},{0,32},{16,48},{32,64},{48,80},{64,96},{80,112},{... | collective-permute-start | bytes 12296 | tf_op jit(solution)/shard_map/ppermute | solution.py:10
  305.1 19.5 %collective-permute-start.17 = (f32[1024]{0:T(1024)S(1)}, f32[1024]{0:T(1024)S(1)}, u32[]{:S(2)}, u32[]{:S(2)}) collective-permute-start(f32[1024]{0:T(1024)S(1)} %broadcast_select_fusion.12), channel_id=1, source_target_pairs={{448,0},{464,16},{480,32},{496,48},{0,64},{16,80},{32,96},{48,112}... | collective-permute-start | bytes 12296 | tf_op jit(solution)/shard_map/ppermute | solution.py:10
  324.5 9.4 %collective-permute-start.18 = (f32[1024]{0:T(1024)S(1)}, f32[1024]{0:T(1024)S(1)}, u32[]{:S(2)}, u32[]{:S(2)}) collective-permute-start(f32[1024]{0:T(1024)S(1)} %broadcast_select_fusion.15), channel_id=1, source_target_pairs={{384,0},{400,16},{416,32},{432,48},{448,64},{464,80},{480,96},{496... | collective-permute-start | bytes 12296 | tf_op jit(solution)/shard_map/ppermute | solution.py:10
  333.9 7.0 %collective-permute-start.19 = (f32[1024]{0:T(1024)S(1)}, f32[1024]{0:T(1024)S(1)}, u32[]{:S(2)}, u32[]{:S(2)}) collective-permute-start(f32[1024]{0:T(1024)S(1)} %broadcast_select_fusion.18), channel_id=1, source_target_pairs={{256,0},{272,16},{288,32},{304,48},{320,64},{336,80},{352,96},{368... | collective-permute-start | bytes 12296 | tf_op jit(solution)/shard_map/ppermute | solution.py:10
Sparse Core Ops, SparseCore 0:
  330.8 135.8 all-reduce.1
where the time goes:
time: 477 us; the launch traced here: 476 us
  waiting for transfers between devices  256 us (54%)
  starting transfers between devices  94.5 us (20%)
  blocking collectives  65.9 us (14%)
  matrix products  18.2 us (4%)
  between operations  14.5 us (3%)
  other arithmetic  13.8 us (3%)
  local copies, waits for them, and re-layouts  12 us (3%)
    ppermute x25, waiting for transfers between devices, shifted(): return lax.ppermute(block, axis, route)  162 us
    ppermute x25, starting transfers between devices, shifted(): return lax.ppermute(block, axis, route)  94.5 us
    psum x1, waiting for transfers between devices, shards(): second, numerator = lax.psum((second_local, numer_local), 'rep')  93.9 us
    psum x1, blocking collectives, shards(): first_sum = lax.psum(first_local, 'rep')  35.3 us
    psum x1, blocking collectives, shards(): second, numerator = lax.psum((second_local, numer_local), 'rep')  30.6 us
    dot_general x32, matrix products, col_step(): lax.dot_general(part_x, other_x, (((1,), (1,)), ((), ())), preferred_elem...  10.9 us
  transfers between devices with their start and end apart: 26, of which 23 were waited for; matrix products, arithmetic and copies ran while one was open for 5% of the time, Pallas kernels for 0%

commit v1 on v0

v1 whole, which is shorter than its diff:
```python
import jax
import jax.numpy as jnp
from jax import lax
from jax.sharding import PartitionSpec as P


def shards(points):
    rows, width = points.shape
    replicas = lax.axis_size("rep")
    teams = lax.axis_size("team")
    part = rows // replicas
    replica = lax.axis_index("rep")
    log_count = jnp.log(jnp.float32(rows * teams))

    mine = lax.dynamic_slice_in_dim(points, replica * part, part, 0)
    cols = lax.all_gather(mine, "team", axis=0, tiled=True)
    half_rows = 0.5 * jnp.sum(jnp.square(points.astype(jnp.float32)), axis=1)
    half_cols = 0.5 * jnp.sum(jnp.square(cols.astype(jnp.float32)), axis=1)
    products = lax.dot_general(
        points, cols, (((1,), (1,)), ((), ())), preferred_element_type=jnp.float32
    )
    cost = half_rows[:, None] + half_cols[None, :] - products
    first = lax.psum(jnp.sum(jnp.exp(cost * -0.25), axis=1), "rep")
    pot_one = -2.0 * (jnp.log(first) - log_count)
    pot_mine = lax.dynamic_slice_in_dim(pot_one, replica * part, part, 0)
    pot_cols = lax.all_gather(pot_mine, "team", axis=0, tiled=True)
    kernel = jnp.exp((pot_cols[None, :] - cost) * 0.5)
    second_part = jnp.sum(kernel, axis=1)
    numer_part = jnp.dot(
        kernel.astype(jnp.bfloat16), cols, preferred_element_type=jnp.float32
    )
    second, numer = lax.psum((second_part, numer_part), "rep")
    potential = 0.5 * (pot_one - 2.0 * (jnp.log(second) - log_count))
    displacement = points.astype(jnp.float32) - numer / second[:, None]
    return (potential, displacement)


def solution(mesh):
    return jax.shard_map(
        shards,
        mesh=mesh,
        in_specs=(P("team", None),),
        out_specs=(P("team"), P("team", None)),
        check_vma=False,
    )
```

time: 477 us -> 314 us (0.66)
  the two profiles are of different devices: /device:TPU:56 before, /device:TPU:8 now
where the time goes in v1:
time: 314 us; the launch traced here: 313 us
  blocking collectives  175 us (56%)
  waiting for transfers between devices  103 us (33%)
  between operations  14.7 us (5%)
  matrix products  10.6 us (3%)
  other arithmetic  8.71 us (3%)
    psum x1, waiting for transfers between devices, shards(): second, numer = lax.psum((second_part, numer_part), 'rep')  103 us
    unnamed x1, blocking collectives  64.4 us
    all_gather x1, blocking collectives, shards(): cols = lax.all_gather(mine, 'team', axis=0, tiled=True)  43.6 us
    psum x1, blocking collectives, shards(): first = lax.psum(jnp.sum(jnp.exp(cost * -0.25), axis=1), 'rep')  36 us
    psum x1, blocking collectives, shards(): second, numer = lax.psum((second_part, numer_part), 'rep')  30.6 us
  transfers between devices with their start and end apart: 1, of which 1 were waited for; matrix products, arithmetic and copies ran while one was open for 2% of the time, Pallas kernels for 0%

profile of v1, /device:TPU:8, one launch (start us, length us, event | category | flops | bytes accessed | tf_op | source)
XLA Modules:
  0.0 313.4 jit_solution(10755890835442421011)
XLA Ops:
  7.2 0.0 all-reduce.3.cloned.1.call-start
  7.2 1.2 fusion.4
  8.4 0.7 constant_dynamic-slice_fusion
  9.1 43.6 %all_gather.6 = bf16[2048,128]{1,0:T(8,128)(2,1)S(1)} all-gather(bf16[64,128]{1,0:T(8,128)(2,1)S(1)} %constant_dynamic-slice_fusion), channel_id=1, replica_groups=mesh['team'=32,'rep'=16] {'team'}, dimensions={0}, use_global_device_ids=true | all-gather | bytes 540672 | tf_op jit(solution)/shard_map/all_gather | solution.py:16
  52.7 0.3 multiply_reduce_fusion
  53.0 5.1 %exponential_reduce_fusion = (f32[1024]{0:T(1024)S(1)}, f32[2048,1024]{1,0:T(8,128)}) fusion(f32[2048]{0:T(1024)S(1)} %broadcast_multiply_fusion, f32[1024]{0:T(1024)S(1)} %broadcast_multiply_fusion.1, bf16[2048,128]{1,0:T(8,128)(2,1)S(1)} %all_gather.6, bf16[1024,128]{1,0:T(8,128)(2,1)} %param.1), kind=kOutput, calls=%fused_computation.2 | convolution fusion | flops 545258496 | bytes 9191424 | tf_op jit(solution)/shard_map/dot_general | solution.py:19
  58.1 36.0 %psum.21 = f32[1024]{0:T(1024)S(1)} all-reduce(f32[1024]{0:T(1024)S(1)} %get-tuple-element.2), channel_id=1, replica_groups=mesh['team'=32,'rep'=16] {'rep'}, use_global_device_ids=true, to_apply=%region_3.0 | all-reduce | flops 1024 | bytes 8192 | tf_op jit(solution)/shard_map/psum | solution.py:23
  94.1 1.3 dynamic-slice
  96.0 0.2 dynamic-slice_dynamic-update-slice_fusion
  96.2 64.4 %all-reduce = f32[2048]{0:T(1024)S(1)} all-reduce(f32[2048]{0:T(1024)S(1)} %dynamic-slice_dynamic-update-slice_fusion), channel_id=1, replica_groups=mesh['team'=32,'rep'=16] {'team'}, use_global_device_ids=true, to_apply=%add | all-reduce | flops 2048 | bytes 16384
  160.6 5.5 %fusion.2 = f32[1024,128]{1,0:T(8,128)} fusion(bf16[2048,128]{1,0:T(8,128)(2,1)S(1)} %all_gather.6, f32[2048,1024]{1,0:T(8,128)} %get-tuple-element.3, f32[2048]{0:T(1024)S(1)} %all-reduce, f32[2048]{0:T(1024)S(1)} %broadcast_multiply_fusion, f32[1024]{0:T(1024)S(1)} %broadcast_multiply_fusion.1), kind=kOutput, calls=%fused_computation.5 | convolution fusion | flops 547356672 | bytes 9457664 | tf_op jit(solution)/shard_map/dot_general | solution.py:29
  166.1 0.0 copy-start
  166.1 0.0 all-reduce.3.cloned.1.call-update
  166.2 4.5 %fusion.1 = f32[1024]{0:T(1024)S(1)} fusion(f32[2048,1024]{1,0:T(8,128)} %get-tuple-element.3, f32[2048]{0:T(1024)S(1)} %all-reduce, f32[2048]{0:T(1024)S(1)} %broadcast_multiply_fusion, f32[1024]{0:T(1024)S(1)} %broadcast_multiply_fusion.1), kind=kLoop, calls=%fused_computation.4 | loop fusion | flops 10484736 | bytes 8413184 | tf_op jit(solution)/shard_map/reduce_sum | solution.py:28
  170.7 30.6 %psum.22 = f32[1024]{0:T(1024)S(1)} all-reduce(f32[1024]{0:T(1024)S(1)} %fusion.1), channel_id=1, replica_groups=mesh['team'=32,'rep'=16] {'rep'}, use_global_device_ids=true, to_apply=%region_5.0 | all-reduce | flops 1024 | bytes 8192 | tf_op jit(solution)/shard_map/psum | solution.py:32
  201.3 0.6 subtract_multiply_fusion
  202.0 102.5 %all-reduce.3.cloned.1.call-done = f32[1024,128]{1,0:T(8,128)} async-done(((f32[1024,128]{1,0:T(8,128)}), f32[1024,128]{1,0:T(8,128)}) %all-reduce.3.cloned.1.call-update) | async-done | bytes 524304 | tf_op jit(solution)/shard_map/psum | solution.py:32
  304.5 0.0 copy-done
  304.5 2.0 convert_subtract_fusion
  (4 shorter events, 0.0 us)
Async XLA Ops:
  7.2 297.3 %all-reduce.3.cloned.1.call-start = ((), (), s32[]{:S(2)}) async-start(), calls=%async_computation | async-start | bytes 1048576 | tf_op jit(solution)/shard_map/psum | solution.py:32
  166.1 138.3 %copy-start = (bf16[1024,128]{1,0:T(8,128)(2,1)S(1)}, bf16[1024,128]{1,0:T(8,128)(2,1)}, u32[]{:S(2)}) copy-start(bf16[1024,128]{1,0:T(8,128)(2,1)} %param.1) | copy-start | bytes 786436
Sparse Core Ops, SparseCore 0:
  166.3 138.1 all-reduce.2

commit v2 on v1

v2 whole, which is shorter than its diff:
```python
import functools
import math

import jax
import jax.numpy as jnp
from jax import lax
from jax.experimental import pallas as pl
from jax.experimental.pallas import tpu as pltpu
from jax.sharding import PartitionSpec as P

LANES = 128
PART = 64
MESH = pl.DeviceIdType.MESH
LOG2E = math.log2(math.e)


def split3(value):
    high = value.astype(jnp.bfloat16).astype(jnp.float32)
    rest = value - high
    mid = rest.astype(jnp.bfloat16).astype(jnp.float32)
    return high, mid, rest - mid


def extra_lanes(block, first, ones):
    wide = block.astype(jnp.float32)
    half = -0.5 * jnp.sum(wide * wide, axis=1, keepdims=True)
    high, mid, low = split3(half)
    lane = lax.broadcasted_iota(jnp.int32, wide.shape, 1)
    extra = jnp.where((lane >= ones) & (lane < ones + 3), 1.0, 0.0)
    extra = jnp.where(lane == first, high, extra)
    extra = jnp.where(lane == first + 1, mid, extra)
    extra = jnp.where(lane == first + 2, low, extra)
    return extra.astype(jnp.bfloat16)


def row_of(acc):
    size = acc.shape[0]
    total = jnp.sum(acc, axis=1, keepdims=True)
    lane = lax.broadcasted_iota(jnp.int32, (size, LANES), 1)
    sub = lax.broadcasted_iota(jnp.int32, (size, LANES), 0)
    return jnp.sum(jnp.where(lane == sub, total, 0.0), axis=0, keepdims=True)


def body(
    teams, reps, pts, pot_out, disp_out,
    rows_aug, cols, cols_aug, sum_one, got_one, pot_mine, pot_cols, pot_rows,
    sum_two, got_two, numer, got_numer, disp_mine, pot_all,
    send_sem, local_sem, rv_pts, rv_one, rv_pot, rv_two, rv_num, rv_disp, rv_fin,
):
    rows = pts.shape[0]
    blocks = rows // LANES
    ncols = teams * PART
    log_count = math.log(rows * teams)
    t = lax.axis_index("team")
    r = lax.axis_index("rep")
    half = lax.rem(r, 2)
    nt = (((1,), (1,)), ((), ()))

    def team_peer(k):
        return lax.rem(t + k, teams)

    def rep_peer(k):
        return lax.rem(r + k, reps)

    def part_at(index):
        return pl.ds(pl.multiple_of(index * PART, PART), PART)

    def block_at(index):
        return pl.ds(pl.multiple_of(index * LANES, LANES), LANES)

    def remote(src, dst, send, recv, where):
        return pltpu.make_async_remote_copy(
            src_ref=src, dst_ref=dst, send_sem=send, recv_sem=recv,
            device_id=where, device_id_type=MESH,
        )

    def each(count, step):
        lax.fori_loop(1, count, lambda k, c: (step(k), c)[1], 0)

    barrier = pltpu.get_barrier_semaphore()

    def greet_team(k):
        pl.semaphore_signal(barrier, 1, device_id={"team": team_peer(k)}, device_id_type=MESH)

    def greet_rep(k):
        pl.semaphore_signal(barrier, 1, device_id={"rep": rep_peer(k)}, device_id_type=MESH)

    each(teams, greet_team)
    each(reps, greet_rep)

    cols[part_at(t), :] = pts[part_at(r), :]

    def widen_rows(b, carry):
        block = pts[block_at(b), :]
        rows_aug[block_at(b), pl.ds(0, LANES)] = block
        rows_aug[block_at(b), pl.ds(LANES, LANES)] = extra_lanes(block, 0, 3)
        return carry

    lax.fori_loop(0, blocks, widen_rows, 0)
    pl.semaphore_wait(barrier, teams + reps - 2)

    def points_copy(k, owner):
        return remote(
            pts.at[part_at(r), :], cols.at[part_at(owner), :],
            send_sem.at[0], rv_pts.at[owner], {"team": team_peer(k)},
        )

    each(teams, lambda k: points_copy(k, t).start())
    each(teams, lambda k: points_copy(k, team_peer(k)).wait_recv())

    def widen_cols(b, carry):
        block = cols[block_at(b), :]
        cols_aug[block_at(b), pl.ds(0, LANES)] = block
        cols_aug[block_at(b), pl.ds(LANES, LANES)] = extra_lanes(block, 3, 0)
        return carry

    lax.fori_loop(0, ncols // LANES, widen_cols, 0)

    def first_block(b, carry):
        mine = rows_aug[block_at(b), :]
        acc = jnp.zeros((LANES, LANES), jnp.float32)
        for s in range(ncols // 256):
            tile = lax.dot_general(
                mine, cols_aug[pl.ds(s * 256, 256), :], nt, preferred_element_type=jnp.float32
            )
            tile = jnp.exp2(tile * (0.25 * LOG2E))
            acc = acc + tile[:, :LANES] + tile[:, LANES:]
        sum_one[b] = row_of(acc)
        return carry

    lax.fori_loop(0, blocks, first_block, 0)

    def one_copy(k, owner):
        return remote(
            sum_one.at[rep_peer(k) // 2], got_one.at[owner],
            send_sem.at[1], rv_one.at[owner], {"rep": rep_peer(k)},
        )

    each(reps, lambda k: one_copy(k, r).start())
    got_one[r] = sum_one[r // 2]
    each(reps, lambda k: one_copy(k, rep_peer(k)).wait_recv())
    first = got_one[0]
    for q in range(1, reps):
        first = first + got_one[q]
    pot_one = -2.0 * (jnp.log(first) - log_count)
    pot_mine[0] = pot_one

    def pot_copy(k, owner):
        return remote(
            pot_mine.at[0], pot_cols.at[owner],
            send_sem.at[2], rv_pot.at[owner], {"team": team_peer(k)},
        )

    each(teams, lambda k: pot_copy(k, t).start())
    pot_cols[t] = pot_one
    each(teams, lambda k: pot_copy(k, team_peer(k)).wait_recv())
    low_lane = lax.broadcasted_iota(jnp.int32, (1, LANES), 1) < PART
    upper = half == 1
    for s in range(teams // 2):
        even = pot_cols[2 * s]
        odd = pot_cols[2 * s + 1]
        even = jnp.where(upper, pltpu.roll(even, PART, 1), even)
        odd = jnp.where(upper, odd, pltpu.roll(odd, PART, 1))
        pot_rows[s] = jnp.where(low_lane, even, odd) * (0.5 * LOG2E)

    def two_copy(block, q, owner):
        return remote(
            sum_two.at[block], got_two.at[owner],
            send_sem.at[3], rv_two.at[owner], {"rep": q},
        )

    def numer_copy(q, owner):
        return remote(
            numer.at[part_at(q), :], got_numer.at[owner],
            send_sem.at[4], rv_num.at[owner], {"rep": q},
        )

    def second_block(i, carry):
        b = lax.rem(r // 2 + 1 + i, blocks)
        mine = rows_aug[block_at(b), :]
        acc = jnp.zeros((LANES, LANES), jnp.float32)
        total = jnp.zeros((LANES, LANES), jnp.float32)
        for s in range(ncols // 256):
            tile = lax.dot_general(
                mine, cols_aug[pl.ds(s * 256, 256), :], nt, preferred_element_type=jnp.float32
            )
            left = jnp.exp2(tile[:, :LANES] * (0.5 * LOG2E) + pot_rows[2 * s])
            right = jnp.exp2(tile[:, LANES:] * (0.5 * LOG2E) + pot_rows[2 * s + 1])
            acc = acc + left + right
            rounded = jnp.concatenate(
                [left.astype(jnp.bfloat16), right.astype(jnp.bfloat16)], axis=1
            )
            total = total + jnp.dot(
                rounded, cols[pl.ds(s * 256, 256), :], preferred_element_type=jnp.float32
            )
        numer[block_at(b), :] = total
        sum_two[b] = row_of(acc)
        for h in range(2):
            q = 2 * b + h

            @pl.when(q != r)
            def _():
                two_copy(b, q, r).start()
                numer_copy(q, r).start()

        return carry

    lax.fori_loop(0, blocks, second_block, 0)
    got_two[r] = sum_two[r // 2]
    got_numer[r] = numer[part_at(r), :]
    each(reps, lambda k: two_copy(0, rep_peer(k), rep_peer(k)).wait_recv())
    second = got_two[0]
    for q in range(1, reps):
        second = second + got_two[q]
    pot_all[r] = 0.5 * (pot_one - 2.0 * (jnp.log(second) - log_count))

    def fin_copy(k, owner):
        return remote(
            pot_all.at[r], pot_all.at[owner],
            send_sem.at[5], rv_fin.at[owner], {"rep": rep_peer(k)},
        )

    each(reps, lambda k: fin_copy(k, r).start())
    lane = lax.broadcasted_iota(jnp.int32, (PART, LANES), 1)
    sub = lax.broadcasted_iota(jnp.int32, (PART, LANES), 0)
    divisor = jnp.sum(jnp.where(lane == sub + half * PART, second, 0.0), axis=1, keepdims=True)
    each(reps, lambda k: numer_copy(rep_peer(k), rep_peer(k)).wait_recv())
    weighted = got_numer[0]
    for q in range(1, reps):
        weighted = weighted + got_numer[q]
    disp_mine[...] = pts[part_at(r), :].astype(jnp.float32) - weighted / divisor

    def disp_copy(k, owner):
        return remote(
            disp_mine, disp_out.at[part_at(owner), :],
            send_sem.at[6], rv_disp.at[owner], {"rep": rep_peer(k)},
        )

    each(reps, lambda k: disp_copy(k, r).start())
    keep = pltpu.make_async_copy(disp_mine, disp_out.at[part_at(r), :], local_sem)
    keep.start()
    each(reps, lambda k: fin_copy(k, rep_peer(k)).wait_recv())
    for b in range(blocks):
        pot_out[b] = pot_all[2 * b]
    each(teams, lambda k: points_copy(k, t).wait_send())
    each(reps, lambda k: one_copy(k, r).wait_send())
    each(teams, lambda k: pot_copy(k, t).wait_send())
    each(reps, lambda k: two_copy(0, rep_peer(k), r).wait_send())
    each(reps, lambda k: numer_copy(rep_peer(k), r).wait_send())
    each(reps, lambda k: fin_copy(k, r).wait_send())
    each(reps, lambda k: disp_copy(k, r).wait_send())
    each(reps, lambda k: disp_copy(k, rep_peer(k)).wait_recv())
    keep.wait()


def shards(points):
    rows, width = points.shape
    teams = lax.axis_size("team")
    reps = lax.axis_size("rep")
    blocks = rows // LANES
    f32 = jnp.float32
    dma = pltpu.SemaphoreType.DMA
    vmem = pltpu.VMEM
    potential, displacement = pl.pallas_call(
        functools.partial(body, teams, reps),
        out_shape=(
            jax.ShapeDtypeStruct((blocks, 1, LANES), f32),
            jax.ShapeDtypeStruct((rows, width), f32),
        ),
        in_specs=[pl.BlockSpec(memory_space=pltpu.VMEM)],
        out_specs=(
            pl.BlockSpec(memory_space=pltpu.VMEM),
            pl.BlockSpec(memory_space=pl.ANY),
        ),
        scratch_shapes=[
            vmem((rows, 2 * width), jnp.bfloat16),
            vmem((teams * PART, width), jnp.bfloat16),
            vmem((teams * PART, 2 * width), jnp.bfloat16),
            vmem((blocks, 1, LANES), f32),
            vmem((reps, 1, LANES), f32),
            vmem((1, 1, LANES), f32),
            vmem((teams, 1, LANES), f32),
            vmem((teams // 2, 1, LANES), f32),
            vmem((blocks, 1, LANES), f32),
            vmem((reps, 1, LANES), f32),
            vmem((rows, width), f32),
            vmem((reps, PART, width), f32),
            vmem((PART, width), f32),
            vmem((reps, 1, LANES), f32),
            dma((7,)),
            dma,
            dma((teams,)),
            dma((reps,)),
            dma((teams,)),
            dma((reps,)),
            dma((reps,)),
            dma((reps,)),
            dma((reps,)),
        ],
        compiler_params=pltpu.CompilerParams(collective_id=0, has_side_effects=True),
    )(points)
    return potential.reshape(rows), displacement


def solution(mesh):
    return jax.shard_map(
        shards,
        mesh=mesh,
        in_specs=(P("team", None),),
        out_specs=(P("team"), P("team", None)),
        check_vma=False,
    )
```

time: 314 us -> 85.8 us (0.27)
  the two profiles are of different devices: /device:TPU:8 before, /device:TPU:1 now
where the time goes in v2:
time: 85.8 us; the launch traced here: 85.6 us
  Pallas kernels  81.8 us (95%)
  local copies, waits for them, and re-layouts  3.14 us (4%)
    pallas_call x1, Pallas kernels, shards(): pl.pallas_call(functools.partial(body, teams, reps), out_shape=(jax.Shape...  81.8 us
    unnamed x4, local copies, waits for them, and re-layouts  3.14 us

profile of v2, /device:TPU:1, one launch (start us, length us, event | category | flops | bytes accessed | tf_op | source)
XLA Modules:
  0.0 85.6 jit_solution(7434473433272439842)
XLA Ops:
  0.6 81.8 %shard_map.30 = (f32[8,1,128]{2,1,0:T(1,128)}, f32[1024,128]{1,0:T(8,128)}) custom-call(bf16[1024,128]{1,0:T(8,128)(2,1)} %pts.1), custom_call_target="tpu_custom_call" | custom-call | tf_op jit(solution)/shard_map/pallas_call | solution.py:264
  82.4 0.0 copy-start
  82.4 0.7 copy-done
  83.1 0.6 copy.5
  83.7 1.9 %copy.6 = f32[1024,128]{1,0:T(8,128)} copy(f32[1024,128]{1,0:T(8,128)} %get-tuple-element.9) | data formatting | bytes 1048576
Async XLA Ops:
  82.4 0.7 copy-start

commit v3 on v2

v3 whole, which is shorter than its diff:
```python
import functools
import math

import jax
import jax.numpy as jnp
from jax import lax
from jax.experimental import pallas as pl
from jax.experimental.pallas import tpu as pltpu
from jax.sharding import PartitionSpec as P

LANES = 128
PART = 64
MESH = pl.DeviceIdType.MESH
LOG2E = math.log2(math.e)


def split3(value):
    high = value.astype(jnp.bfloat16).astype(jnp.float32)
    rest = value - high
    mid = rest.astype(jnp.bfloat16).astype(jnp.float32)
    return high, mid, rest - mid


def extra_lanes(block, first, ones):
    wide = block.astype(jnp.float32)
    half = -0.5 * jnp.sum(wide * wide, axis=1, keepdims=True)
    high, mid, low = split3(half)
    lane = lax.broadcasted_iota(jnp.int32, wide.shape, 1)
    extra = jnp.where((lane >= ones) & (lane < ones + 3), 1.0, 0.0)
    extra = jnp.where(lane == first, high, extra)
    extra = jnp.where(lane == first + 1, mid, extra)
    extra = jnp.where(lane == first + 2, low, extra)
    return extra.astype(jnp.bfloat16)


def row_of(acc):
    size = acc.shape[0]
    total = jnp.sum(acc, axis=1, keepdims=True)
    lane = lax.broadcasted_iota(jnp.int32, (size, LANES), 1)
    sub = lax.broadcasted_iota(jnp.int32, (size, LANES), 0)
    return jnp.sum(jnp.where(lane == sub, total, 0.0), axis=0, keepdims=True)


def body(
    teams, reps, pts, pot_out, disp_out,
    rows_aug, cols, expo, part_one, sib_one, chip_one, got_one, pot, pot_scaled,
    numer, sum_two, far_numer, far_two, got_numer, got_two, disp_mine, pot_all,
    send_sem, local_sem, rv_pts, rv_fwd, rv_sib, rv_one, rv_pot,
    rv_xnum, rv_xtwo, rv_num, rv_two, rv_disp, rv_side, rv_fin,
):
    rows = pts.shape[0]
    blocks = rows // LANES
    ncols = teams * PART
    chunks = ncols // 256
    depth = reps // 2
    half_blocks = blocks // 2
    log_count = math.log(rows * teams)
    t = lax.axis_index("team")
    r = lax.axis_index("rep")
    core = lax.rem(t, 2)
    sibling = t + 1 - 2 * core
    near = r // depth
    z = lax.rem(r, depth)
    across = lax.rem(r + depth, reps)
    pairs = chunks // 2
    home = t // 4
    nt = (((1,), (1,)), ((), ()))

    def part_at(index):
        return pl.ds(pl.multiple_of(index * PART, PART), PART)

    def block_at(index):
        return pl.ds(pl.multiple_of(index * LANES, LANES), LANES)

    def chunk_at(index):
        return pl.ds(pl.multiple_of(index * 256, 256), 256)

    def remote(src, dst, send, recv, where):
        return pltpu.make_async_remote_copy(
            src_ref=src, dst_ref=dst, send_sem=send, recv_sem=recv,
            device_id=where, device_id_type=MESH,
        )

    def each(first, count, step):
        lax.fori_loop(first, count, lambda k, c: (step(k), c)[1], 0)

    def same_core(k):
        return lax.rem(t + 2 * k, teams)

    def rep_peer(k):
        return lax.rem(r + k, reps)

    def z_peer(k):
        return near * depth + lax.rem(z + k, depth)

    def chunk_of(i):
        side, step = lax.rem(i, 2), i // 2
        step = step + (step // 2) * (1 - 2 * lax.rem(step, 2))
        return lax.rem(home // pairs + side, 2) * pairs + lax.rem(home + step, pairs)

    chips = teams // 2
    pend = []

    def finish():
        for step in pend:
            step()

    barrier = pltpu.get_barrier_semaphore()

    def greet(where):
        pl.semaphore_signal(barrier, 1, device_id=where, device_id_type=MESH)

    each(1, chips, lambda k: greet({"team": same_core(k)}))
    greet({"team": sibling})
    each(1, reps, lambda k: greet({"rep": rep_peer(k)}))
    own = pltpu.make_async_copy(pts.at[part_at(r), :], cols.at[part_at(t), :], local_sem)
    own.start()
    pl.semaphore_wait(barrier, chips + reps - 1)

    def points_copy(owner, target):
        return remote(
            pts.at[part_at(r), :], cols.at[part_at(owner), :],
            send_sem.at[0], rv_pts.at[owner], {"team": target},
        )

    def forward_copy(owner):
        return remote(
            cols.at[part_at(owner), :], cols.at[part_at(owner), :],
            send_sem.at[1], rv_fwd.at[owner], {"team": sibling},
        )

    def send_points(i, carry):
        for h in range(2):
            q = 4 * chunk_of(i) + 2 * h + core

            @pl.when(q != t)
            def _():
                points_copy(t, q).start()

        return carry

    lax.fori_loop(0, chunks, send_points, 0)
    pend.append(lambda: each(1, chips, lambda k: points_copy(t, t).wait_send()))
    own.wait()

    def widen_rows(b, carry):
        block = pts[block_at(b), :]
        rows_aug[block_at(b), pl.ds(0, LANES)] = block
        rows_aug[block_at(b), pl.ds(LANES, LANES)] = extra_lanes(block, 0, 3)
        return carry

    lax.fori_loop(0, blocks, widen_rows, 0)

    def relay_chunk(i):
        for h in range(2):
            q = 4 * chunk_of(i) + 2 * h + core

            @pl.when(q != t)
            def _():
                points_copy(q, q).wait_recv()

            forward_copy(q).start()

    pend.append(lambda: each(0, chips, lambda k: forward_copy(t).wait_send()))

    def sib_copy(c, src):
        return remote(
            part_one.at[src], sib_one.at[c], send_sem.at[2], rv_sib.at[c], {"team": sibling}
        )

    def first_chunk(i, carry):
        c = chunk_of(i)

        @pl.when(i + 1 < chunks)
        def _():
            relay_chunk(i + 1)

        for h in range(2):
            forward_copy(4 * c + 2 * h + 1 - core).wait_recv()
        block = cols[chunk_at(c), :]
        extra = extra_lanes(block, 3, 0)
        wide = jnp.concatenate([block, extra], axis=1)
        acc = jnp.zeros((1, 256), jnp.float32)
        for b in range(max(rows // 256, 1)):
            size = min(rows, 256)
            tile = lax.dot_general(
                rows_aug[pl.ds(b * size, size), :], wide, nt, preferred_element_type=jnp.float32
            )
            tile = tile * (0.5 * LOG2E)
            expo[pl.ds(b * size, size), chunk_at(c)] = tile
            acc = acc + jnp.sum(jnp.exp2(0.5 * tile), axis=0, keepdims=True)
        part_one[2 * c] = acc[:, :LANES]
        part_one[2 * c + 1] = acc[:, LANES:]
        sib_copy(c, 2 * c + 1 - core).start()
        return carry

    relay_chunk(0)
    lax.fori_loop(0, chunks, first_chunk, 0)
    pend.append(lambda: each(0, chunks, lambda c: sib_copy(c, 2 * c).wait_send()))

    def add_sibling(c, carry):
        sib_copy(c, 2 * c).wait_recv()
        chip_one[pl.ds(c, 1), :] = part_one[2 * c + core] + sib_one[c]
        return carry

    lax.fori_loop(0, chunks, add_sibling, 0)

    def one_copy(owner, target):
        return remote(
            chip_one, got_one.at[owner], send_sem.at[3], rv_one.at[owner], {"team": target}
        )

    each(1, chips, lambda k: one_copy(t // 2, same_core(k)).start())
    pend.append(lambda: each(1, chips, lambda k: one_copy(0, t).wait_send()))
    got_one[t // 2] = chip_one[...]
    each(1, chips, lambda k: one_copy(same_core(k) // 2, t).wait_recv())
    first = got_one[0]
    for q in range(1, chips):
        first = first + got_one[q]
    pot[core] = -2.0 * (jnp.log(first) - log_count)

    def pot_copy(owner):
        return remote(
            pot.at[owner], pot.at[owner], send_sem.at[4], rv_pot, {"team": sibling}
        )

    pot_copy(core).start()
    pend.append(lambda: pot_copy(core).wait_send())
    pot_copy(1 - core).wait_recv()
    pot_scaled[...] = pot[...] * (0.5 * LOG2E)

    def second_block(b):
        acc = jnp.zeros((LANES, LANES), jnp.float32)
        total = jnp.zeros((LANES, LANES), jnp.float32)
        for s in range(chunks):
            tile = expo[block_at(b), pl.ds(s * 256, 256)]
            left = jnp.exp2(tile[:, :LANES] + pot_scaled[0, s : s + 1, :])
            right = jnp.exp2(tile[:, LANES:] + pot_scaled[1, s : s + 1, :])
            acc = acc + left + right
            rounded = jnp.concatenate(
                [left.astype(jnp.bfloat16), right.astype(jnp.bfloat16)], axis=1
            )
            total = total + jnp.dot(
                rounded, cols[pl.ds(s * 256, 256), :], preferred_element_type=jnp.float32
            )
        return row_of(acc), total

    def xnum_copy(b, slot):
        return remote(
            numer.at[block_at(b), :], far_numer.at[slot],
            send_sem.at[5], rv_xnum.at[slot], {"rep": across},
        )

    def xtwo_copy(b, slot):
        return remote(
            sum_two.at[b], far_two.at[slot],
            send_sem.at[6], rv_xtwo.at[slot], {"rep": across},
        )

    def turn(i):
        return lax.rem(z // 2 + 1 + i, half_blocks)

    def far_block(i, carry):
        slot = turn(i)
        b = (1 - near) * half_blocks + slot
        row, total = second_block(b)
        numer[block_at(b), :] = total
        sum_two[b] = row
        xnum_copy(b, slot).start()
        xtwo_copy(b, slot).start()
        return carry

    lax.fori_loop(0, half_blocks, far_block, 0)
    pend.append(lambda: each(0, half_blocks, lambda k: xnum_copy(k, k).wait_send()))
    pend.append(lambda: each(0, half_blocks, lambda k: xtwo_copy(k, k).wait_send()))

    def num_copy(dest, owner):
        return remote(
            numer.at[part_at(dest), :], got_numer.at[owner],
            send_sem.at[7], rv_num.at[owner], {"rep": dest},
        )

    def two_copy(b, dest, owner):
        return remote(
            sum_two.at[b], got_two.at[owner],
            send_sem.at[8], rv_two.at[owner], {"rep": dest},
        )

    def near_block(i, carry):
        slot = turn(i)
        b = near * half_blocks + slot
        row, total = second_block(b)
        xnum_copy(b, slot).wait_recv()
        xtwo_copy(b, slot).wait_recv()
        numer[block_at(b), :] = total + far_numer[slot]
        sum_two[b] = row + far_two[slot]
        for h in range(2):
            q = 2 * b + h

            @pl.when(q != r)
            def _():
                two_copy(b, q, z).start()
                num_copy(q, z).start()

        return carry

    lax.fori_loop(0, half_blocks, near_block, 0)
    pend.append(lambda: each(1, depth, lambda k: num_copy(r, z).wait_send()))
    pend.append(lambda: each(1, depth, lambda k: two_copy(0, r, z).wait_send()))
    got_two[z] = sum_two[r // 2]
    got_numer[z] = numer[part_at(r), :]
    each(1, depth, lambda k: two_copy(0, r, lax.rem(z + k, depth)).wait_recv())
    second = got_two[0]
    for q in range(1, depth):
        second = second + got_two[q]
    half = lax.rem(r, 2)
    pot_own = pot[lax.rem(t // 2, 2), pl.ds(home, 1), :]
    pot_own = jnp.where(half == core, pot_own, pltpu.roll(pot_own, PART, 1))
    pot_all[r] = 0.5 * (pot_own - 2.0 * (jnp.log(second) - log_count))

    def fin_copy(owner, target):
        return remote(
            pot_all.at[owner], pot_all.at[owner],
            send_sem.at[9], rv_fin.at[owner], {"rep": target},
        )

    each(1, reps, lambda k: fin_copy(r, rep_peer(k)).start())
    pend.append(lambda: each(1, reps, lambda k: fin_copy(r, r).wait_send()))
    lane = lax.broadcasted_iota(jnp.int32, (PART, LANES), 1)
    sub = lax.broadcasted_iota(jnp.int32, (PART, LANES), 0)
    divisor = jnp.sum(jnp.where(lane == sub + half * PART, second, 0.0), axis=1, keepdims=True)
    each(1, depth, lambda k: num_copy(r, lax.rem(z + k, depth)).wait_recv())
    weighted = got_numer[0]
    for q in range(1, depth):
        weighted = weighted + got_numer[q]
    disp_mine[...] = pts[part_at(r), :].astype(jnp.float32) - weighted / divisor

    def disp_copy(owner, target):
        return remote(
            disp_mine, disp_out.at[part_at(owner), :],
            send_sem.at[10], rv_disp.at[owner], {"rep": target},
        )

    def side_copy(owner, src):
        return remote(
            src, disp_out.at[part_at(owner), :],
            send_sem.at[11], rv_side.at[owner], {"rep": across},
        )

    side_copy(r, disp_mine).start()
    each(1, depth, lambda k: disp_copy(r, z_peer(k)).start())
    pend.append(lambda: each(1, depth, lambda k: disp_copy(r, r).wait_send()))
    pend.append(lambda: each(0, depth, lambda k: side_copy(r, disp_mine).wait_send()))
    keep = pltpu.make_async_copy(disp_mine, disp_out.at[part_at(r), :], local_sem)
    keep.start()

    def pass_on(k):
        q = z_peer(k)
        disp_copy(q, r).wait_recv()
        side_copy(q, disp_out.at[part_at(q), :]).start()

    each(1, depth, pass_on)
    each(1, reps, lambda k: fin_copy(rep_peer(k), r).wait_recv())
    low_lane = lax.broadcasted_iota(jnp.int32, (1, LANES), 1) < PART
    for b in range(blocks):
        pot_out[b] = jnp.where(low_lane, pot_all[2 * b], pot_all[2 * b + 1])
    finish()
    each(0, depth, lambda k: side_copy(lax.rem(z_peer(k) + depth, reps), disp_mine).wait_recv())
    keep.wait()


def shards(points):
    rows, width = points.shape
    teams = lax.axis_size("team")
    reps = lax.axis_size("rep")
    blocks = rows // LANES
    chunks = teams * PART // 256
    depth = reps // 2
    f32 = jnp.float32
    dma = pltpu.SemaphoreType.DMA
    vmem = pltpu.VMEM
    potential, displacement = pl.pallas_call(
        functools.partial(body, teams, reps),
        out_shape=(
            jax.ShapeDtypeStruct((blocks, 1, LANES), f32),
            jax.ShapeDtypeStruct((rows, width), f32),
        ),
        in_specs=[pl.BlockSpec(memory_space=pltpu.VMEM)],
        out_specs=(
            pl.BlockSpec(memory_space=pltpu.VMEM),
            pl.BlockSpec(memory_space=pl.ANY),
        ),
        scratch_shapes=[
            vmem((rows, 2 * width), jnp.bfloat16),
            vmem((teams * PART, width), jnp.bfloat16),
            vmem((rows, teams * PART), f32),
            vmem((2 * chunks, 1, LANES), f32),
            vmem((chunks, 1, LANES), f32),
            vmem((chunks, LANES), f32),
            vmem((teams // 2, chunks, LANES), f32),
            vmem((2, chunks, LANES), f32),
            vmem((2, chunks, LANES), f32),
            vmem((rows, width), f32),
            vmem((blocks, 1, LANES), f32),
            vmem((blocks // 2, LANES, width), f32),
            vmem((blocks // 2, 1, LANES), f32),
            vmem((depth, PART, width), f32),
            vmem((depth, 1, LANES), f32),
            vmem((PART, width), f32),
            vmem((reps, 1, LANES), f32),
            dma((12,)),
            dma,
            dma((teams,)),
            dma((teams,)),
            dma((chunks,)),
            dma((teams // 2,)),
            dma,
            dma((blocks // 2,)),
            dma((blocks // 2,)),
            dma((depth,)),
            dma((depth,)),
            dma((reps,)),
            dma((reps,)),
            dma((reps,)),
        ],
        compiler_params=pltpu.CompilerParams(collective_id=0, has_side_effects=True),
    )(points)
    return potential.reshape(rows), displacement


def solution(mesh):
    return jax.shard_map(
        shards,
        mesh=mesh,
        in_specs=(P("team", None),),
        out_specs=(P("team"), P("team", None)),
        check_vma=False,
    )
```

time: 85.8 us -> 68.9 us (0.80)
  Pallas kernels: 81.8 us -> 64 us
    pallas_call x1, Pallas kernels: 81.8 us -> 64 us  [shards(): pl.pallas_call(functools.partial(body, teams, reps), out_shape=(jax.Shape...]
where the time goes in v3:
time: 68.9 us; the launch traced here: 67.8 us
  Pallas kernels  64 us (93%)
  local copies, waits for them, and re-layouts  3.14 us (5%)
    pallas_call x1, Pallas kernels, shards(): pl.pallas_call(functools.partial(body, teams, reps), out_shape=(jax.Shape...  64 us
    unnamed x4, local copies, waits for them, and re-layouts  3.14 us

profile of v3, /device:TPU:1, one launch (start us, length us, event | category | flops | bytes accessed | tf_op | source)
XLA Modules:
  0.0 67.8 jit_solution(12281219313988898431)
XLA Ops:
  0.6 64.0 %shard_map.30 = (f32[8,1,128]{2,1,0:T(1,128)}, f32[1024,128]{1,0:T(8,128)}) custom-call(bf16[1024,128]{1,0:T(8,128)(2,1)} %pts.1), custom_call_target="tpu_custom_call" | custom-call | tf_op jit(solution)/shard_map/pallas_call | solution.py:382
  64.7 0.0 copy-start
  64.7 0.7 copy-done
  65.4 0.6 copy.5
  66.0 1.9 %copy.6 = f32[1024,128]{1,0:T(8,128)} copy(f32[1024,128]{1,0:T(8,128)} %get-tuple-element.9) | data formatting | bytes 1048576
Async XLA Ops:
  64.7 0.7 %copy-start = (f32[8,1,128]{2,1,0:T(1,128)S(1)}, f32[8,1,128]{2,1,0:T(1,128)}, u32[]{:S(2)}) copy-start(f32[8,1,128]{2,1,0:T(1,128)} %get-tuple-element.4) | copy-start | bytes 12292

commit v4 on v3

v4 whole, which is shorter than its diff:
```python
import functools
import math

import jax
import jax.numpy as jnp
from jax import lax
from jax.experimental import pallas as pl
from jax.experimental.pallas import tpu as pltpu
from jax.sharding import PartitionSpec as P

LANES = 128
PART = 64
LEAD = 2
MESH = pl.DeviceIdType.MESH
LOG2E = math.log2(math.e)


def split3(value):
    high = value.astype(jnp.bfloat16).astype(jnp.float32)
    rest = value - high
    mid = rest.astype(jnp.bfloat16).astype(jnp.float32)
    return high, mid, rest - mid


def extra_lanes(block, first, ones):
    wide = block.astype(jnp.float32)
    half = -0.5 * jnp.sum(wide * wide, axis=1, keepdims=True)
    high, mid, low = split3(half)
    lane = lax.broadcasted_iota(jnp.int32, wide.shape, 1)
    extra = jnp.where((lane >= ones) & (lane < ones + 3), 1.0, 0.0)
    extra = jnp.where(lane == first, high, extra)
    extra = jnp.where(lane == first + 1, mid, extra)
    extra = jnp.where(lane == first + 2, low, extra)
    return extra.astype(jnp.bfloat16)


def row_of(acc):
    size = acc.shape[0]
    total = jnp.sum(acc, axis=1, keepdims=True)
    lane = lax.broadcasted_iota(jnp.int32, (size, LANES), 1)
    sub = lax.broadcasted_iota(jnp.int32, (size, LANES), 0)
    return jnp.sum(jnp.where(lane == sub, total, 0.0), axis=0, keepdims=True)


def body(
    teams, reps, pts, pot_out, disp_out,
    mate, rows_aug, cols, expo, chip_one, got_one, pot, pot_scaled,
    out_numer, out_two, sib_numer, sib_two,
    numer, sum_two, far_numer, far_two, got_numer, got_two, disp_mine, pot_all,
    send_sem, local_sem, rv_mate, rv_pts, rv_one, rv_snum, rv_stwo,
    rv_xnum, rv_xtwo, rv_num, rv_two, rv_disp, rv_side, rv_fin,
):
    rows = pts.shape[0]
    blocks = rows // LANES
    chips = teams // 2
    chunks = chips // 2
    depth = reps // 2
    half_blocks = blocks // 2
    log_count = math.log(rows * teams)
    t = lax.axis_index("team")
    r = lax.axis_index("rep")
    core = lax.rem(t, 2)
    sibling = t + 1 - 2 * core
    near = r // depth
    z = lax.rem(r, depth)
    across = lax.rem(r + depth, reps)
    pairs = chunks // 2
    home = t // 4
    nt = (((1,), (1,)), ((), ()))

    def part_at(index):
        return pl.ds(pl.multiple_of(index * PART, PART), PART)

    def block_at(index):
        return pl.ds(pl.multiple_of(index * LANES, LANES), LANES)

    def remote(src, dst, send, recv, where):
        return pltpu.make_async_remote_copy(
            src_ref=src, dst_ref=dst, send_sem=send, recv_sem=recv,
            device_id=where, device_id_type=MESH,
        )

    def each(first, count, step):
        lax.fori_loop(first, count, lambda k, c: (step(k), c)[1], 0)

    def same_core(k):
        return lax.rem(t + 2 * k, teams)

    def rep_peer(k):
        return lax.rem(r + k, reps)

    def z_peer(k):
        return near * depth + lax.rem(z + k, depth)

    def chunk_of(i):
        side, step = lax.rem(i, 2), i // 2
        step = step + (step // 2) * (1 - 2 * lax.rem(step, 2))
        return lax.rem(home // pairs + side, 2) * pairs + lax.rem(home + step, pairs)

    pend = []

    def finish():
        for step in pend:
            step()

    barrier = pltpu.get_barrier_semaphore()

    def greet(where):
        pl.semaphore_signal(barrier, 1, device_id=where, device_id_type=MESH)

    each(1, chips, lambda k: greet({"team": same_core(k)}))
    greet({"team": sibling})
    each(1, reps, lambda k: greet({"rep": rep_peer(k)}))
    own = pltpu.make_async_copy(pts.at[part_at(r), :], cols.at[part_at(t // 2), :], local_sem)
    own.start()
    pl.semaphore_wait(barrier, chips + reps - 1)

    def points_copy(owner, target):
        return remote(
            pts.at[part_at(r), :], cols.at[part_at(owner), :],
            send_sem.at[0], rv_pts.at[owner], {"team": target},
        )

    def send_points(i, carry):
        for h in range(2):
            q = 4 * chunk_of(i) + 2 * h + core

            @pl.when(q != t)
            def _():
                points_copy(t // 2, q).start()

        return carry

    lax.fori_loop(0, chunks, send_points, 0)
    pend.append(lambda: each(1, chips, lambda k: points_copy(t // 2, t).wait_send()))
    mate_copy = remote(pts, mate, send_sem.at[1], rv_mate, {"team": sibling})
    mate_copy.start()
    pend.append(mate_copy.wait_send)
    own.wait()

    def widen_from(ref, first):
        def widen_rows(b, carry):
            block = ref[block_at(b), :]
            rows_aug[block_at(first + b), pl.ds(0, LANES)] = block
            rows_aug[block_at(first + b), pl.ds(LANES, LANES)] = extra_lanes(block, 0, 3)
            return carry

        lax.fori_loop(0, blocks, widen_rows, 0)

    widen_from(pts, 0)
    mate_copy.wait_recv()
    widen_from(mate, blocks)

    def first_chunk(i, carry):
        c = chunk_of(i)
        for h in range(2):
            k = 2 * c + h

            @pl.when(k != t // 2)
            def _():
                points_copy(k, t).wait_recv()

        block = cols[block_at(c), :]
        wide = jnp.concatenate([block, extra_lanes(block, 3, 0)], axis=1)
        acc = jnp.zeros((1, LANES), jnp.float32)
        for b in range(2 * rows // 256):
            tile = lax.dot_general(
                rows_aug[pl.ds(b * 256, 256), :], wide, nt, preferred_element_type=jnp.float32
            )
            tile = tile * (0.5 * LOG2E)
            expo[c, pl.ds(b * 256, 256), :] = tile
            acc = acc + jnp.sum(jnp.exp2(0.5 * tile), axis=0, keepdims=True)
        chip_one[pl.ds(c, 1), :] = acc
        return carry

    lax.fori_loop(0, chunks, first_chunk, 0)

    def one_copy(owner, target):
        return remote(
            chip_one, got_one.at[owner], send_sem.at[3], rv_one.at[owner], {"team": target}
        )

    each(1, chips, lambda k: one_copy(t // 2, same_core(k)).start())
    pend.append(lambda: each(1, chips, lambda k: one_copy(0, t).wait_send()))
    got_one[t // 2] = chip_one[...]
    each(1, chips, lambda k: one_copy(same_core(k) // 2, t).wait_recv())
    first = got_one[0]
    for q in range(1, chips):
        first = first + got_one[q]
    pot[...] = -2.0 * (jnp.log(first) - log_count)

    pot_scaled[...] = pot[...] * (0.5 * LOG2E)

    def second_block(b):
        acc = jnp.zeros((LANES, LANES), jnp.float32)
        total = jnp.zeros((LANES, LANES), jnp.float32)
        for s in range(chunks // 2):
            left = jnp.exp2(expo[2 * s, block_at(b), :] + pot_scaled[2 * s : 2 * s + 1, :])
            right = jnp.exp2(expo[2 * s + 1, block_at(b), :] + pot_scaled[2 * s + 1 : 2 * s + 2, :])
            acc = acc + left + right
            rounded = jnp.concatenate(
                [left.astype(jnp.bfloat16), right.astype(jnp.bfloat16)], axis=1
            )
            total = total + jnp.dot(
                rounded, cols[pl.ds(s * 256, 256), :], preferred_element_type=jnp.float32
            )
        return row_of(acc), total

    def snum_copy(b):
        return remote(
            out_numer.at[b], sib_numer.at[b], send_sem.at[2], rv_snum.at[b], {"team": sibling}
        )

    def stwo_copy(b):
        return remote(
            out_two.at[b], sib_two.at[b], send_sem.at[4], rv_stwo.at[b], {"team": sibling}
        )

    def xnum_copy(b, slot):
        return remote(
            numer.at[block_at(b), :], far_numer.at[slot],
            send_sem.at[5], rv_xnum.at[slot], {"rep": across},
        )

    def xtwo_copy(b, slot):
        return remote(
            sum_two.at[b], far_two.at[slot],
            send_sem.at[6], rv_xtwo.at[slot], {"rep": across},
        )

    def turn(i):
        return lax.rem(z // 2 + 1 + i, half_blocks)

    def num_copy(dest, owner):
        return remote(
            numer.at[part_at(dest), :], got_numer.at[owner],
            send_sem.at[7], rv_num.at[owner], {"rep": dest},
        )

    def two_copy(b, dest, owner):
        return remote(
            sum_two.at[b], got_two.at[owner],
            send_sem.at[8], rv_two.at[owner], {"rep": dest},
        )

    def place(i):
        side, slot = i // half_blocks, turn(lax.rem(i, half_blocks))
        return side, slot, lax.rem(1 - near + side, 2) * half_blocks + slot

    def for_sibling(i):
        b = place(i)[2]
        row, total = second_block(blocks + b)
        out_numer[b] = total
        out_two[b] = row
        snum_copy(b).start()
        stwo_copy(b).start()

    def for_own(i):
        side, slot, b = place(i)
        row, total = second_block(b)
        snum_copy(b).wait_recv()
        stwo_copy(b).wait_recv()
        numer[block_at(b), :] = total + sib_numer[b]
        sum_two[b] = row + sib_two[b]

        @pl.when(side == 0)
        def _():
            xnum_copy(b, slot).start()
            xtwo_copy(b, slot).start()

        @pl.when(side == 1)
        def _():
            xnum_copy(b, slot).wait_recv()
            xtwo_copy(b, slot).wait_recv()
            numer[block_at(b), :] = numer[block_at(b), :] + far_numer[slot]
            sum_two[b] = sum_two[b] + far_two[slot]
            for h in range(2):
                q = 2 * b + h

                @pl.when(q != r)
                def _():
                    two_copy(b, q, z).start()
                    num_copy(q, z).start()

    def second_step(i, carry):
        @pl.when(i < blocks)
        def _():
            for_sibling(i)

        @pl.when(i >= LEAD)
        def _():
            for_own(i - LEAD)

        return carry

    lax.fori_loop(0, blocks + LEAD, second_step, 0)
    pend.append(lambda: each(0, blocks, lambda k: snum_copy(k).wait_send()))
    pend.append(lambda: each(0, blocks, lambda k: stwo_copy(k).wait_send()))
    pend.append(lambda: each(0, half_blocks, lambda k: xnum_copy(k, k).wait_send()))
    pend.append(lambda: each(0, half_blocks, lambda k: xtwo_copy(k, k).wait_send()))
    pend.append(lambda: each(1, depth, lambda k: num_copy(r, z).wait_send()))
    pend.append(lambda: each(1, depth, lambda k: two_copy(0, r, z).wait_send()))
    got_two[z] = sum_two[r // 2]
    got_numer[z] = numer[part_at(r), :]
    each(1, depth, lambda k: two_copy(0, r, lax.rem(z + k, depth)).wait_recv())
    second = got_two[0]
    for q in range(1, depth):
        second = second + got_two[q]
    half = lax.rem(r, 2)
    pot_own = pot[pl.ds(home, 1), :]
    pot_own = jnp.where(half == lax.rem(t // 2, 2), pot_own, pltpu.roll(pot_own, PART, 1))
    pot_all[r] = 0.5 * (pot_own - 2.0 * (jnp.log(second) - log_count))

    def fin_copy(owner, target):
        return remote(
            pot_all.at[owner], pot_all.at[owner],
            send_sem.at[9], rv_fin.at[owner], {"rep": target},
        )

    each(1, reps, lambda k: fin_copy(r, rep_peer(k)).start())
    pend.append(lambda: each(1, reps, lambda k: fin_copy(r, r).wait_send()))
    lane = lax.broadcasted_iota(jnp.int32, (PART, LANES), 1)
    sub = lax.broadcasted_iota(jnp.int32, (PART, LANES), 0)
    divisor = jnp.sum(jnp.where(lane == sub + half * PART, second, 0.0), axis=1, keepdims=True)
    each(1, depth, lambda k: num_copy(r, lax.rem(z + k, depth)).wait_recv())
    weighted = got_numer[0]
    for q in range(1, depth):
        weighted = weighted + got_numer[q]
    disp_mine[...] = pts[part_at(r), :].astype(jnp.float32) - weighted / divisor

    def disp_copy(owner, target):
        return remote(
            disp_mine, disp_out.at[part_at(owner), :],
            send_sem.at[10], rv_disp.at[owner], {"rep": target},
        )

    def side_copy(owner, src, target):
        return remote(
            src, disp_out.at[part_at(owner), :],
            send_sem.at[11], rv_side.at[owner], {"rep": target},
        )

    opposite = lax.rem(z_peer(depth // 2) + depth, reps)
    side_copy(r, disp_mine, opposite).start()
    side_copy(r, disp_mine, across).start()
    each(1, depth, lambda k: disp_copy(r, z_peer(k)).start())
    pend.append(lambda: each(1, depth, lambda k: disp_copy(r, r).wait_send()))
    pend.append(lambda: each(0, depth, lambda k: side_copy(r, disp_mine, across).wait_send()))
    keep = pltpu.make_async_copy(disp_mine, disp_out.at[part_at(r), :], local_sem)
    keep.start()

    def pass_on(k):
        q = z_peer(k)
        disp_copy(q, r).wait_recv()

        @pl.when(k != depth // 2)
        def _():
            side_copy(q, disp_out.at[part_at(q), :], across).start()

    each(1, depth, pass_on)
    each(1, reps, lambda k: fin_copy(rep_peer(k), r).wait_recv())
    low_lane = lax.broadcasted_iota(jnp.int32, (1, LANES), 1) < PART
    for b in range(blocks):
        pot_out[b] = jnp.where(low_lane, pot_all[2 * b], pot_all[2 * b + 1])
    finish()
    each(0, depth, lambda k: side_copy(lax.rem(z_peer(k) + depth, reps), disp_mine, r).wait_recv())
    keep.wait()


def shards(points):
    rows, width = points.shape
    teams = lax.axis_size("team")
    reps = lax.axis_size("rep")
    blocks = rows // LANES
    chips = teams // 2
    chunks = chips // 2
    depth = reps // 2
    f32 = jnp.float32
    dma = pltpu.SemaphoreType.DMA
    vmem = pltpu.VMEM
    potential, displacement = pl.pallas_call(
        functools.partial(body, teams, reps),
        out_shape=(
            jax.ShapeDtypeStruct((blocks, 1, LANES), f32),
            jax.ShapeDtypeStruct((rows, width), f32),
        ),
        in_specs=[pl.BlockSpec(memory_space=pltpu.VMEM)],
        out_specs=(
            pl.BlockSpec(memory_space=pltpu.VMEM),
            pl.BlockSpec(memory_space=pl.ANY),
        ),
        scratch_shapes=[
            vmem((rows, width), jnp.bfloat16),
            vmem((2 * rows, 2 * width), jnp.bfloat16),
            vmem((chips * PART, width), jnp.bfloat16),
            vmem((chunks, 2 * rows, LANES), f32),
            vmem((chunks, LANES), f32),
            vmem((chips, chunks, LANES), f32),
            vmem((chunks, LANES), f32),
            vmem((chunks, LANES), f32),
            vmem((blocks, LANES, width), f32),
            vmem((blocks, 1, LANES), f32),
            vmem((blocks, LANES, width), f32),
            vmem((blocks, 1, LANES), f32),
            vmem((rows, width), f32),
            vmem((blocks, 1, LANES), f32),
            vmem((blocks // 2, LANES, width), f32),
            vmem((blocks // 2, 1, LANES), f32),
            vmem((depth, PART, width), f32),
            vmem((depth, 1, LANES), f32),
            vmem((PART, width), f32),
            vmem((reps, 1, LANES), f32),
            dma((12,)),
            dma,
            dma,
            dma((chips,)),
            dma((chips,)),
            dma((blocks,)),
            dma((blocks,)),
            dma((blocks // 2,)),
            dma((blocks // 2,)),
            dma((depth,)),
            dma((depth,)),
            dma((reps,)),
            dma((reps,)),
            dma((reps,)),
        ],
        compiler_params=pltpu.CompilerParams(collective_id=0, has_side_effects=True),
    )(points)
    return potential.reshape(rows), displacement


def solution(mesh):
    return jax.shard_map(
        shards,
        mesh=mesh,
        in_specs=(P("team", None),),
        out_specs=(P("team"), P("team", None)),
        check_vma=False,
    )
```

time: 68.9 us -> 66.6 us (0.967)
  the two profiles are of different devices: /device:TPU:1 before, /device:TPU:72 now
where the time goes in v4:
time: 66.6 us; the launch traced here: 66.3 us
  Pallas kernels  62.5 us (94%)
  local copies, waits for them, and re-layouts  3.14 us (5%)
    pallas_call x1, Pallas kernels, shards(): pl.pallas_call(functools.partial(body, teams, reps), out_shape=(jax.Shape...  62.5 us
    unnamed x4, local copies, waits for them, and re-layouts  3.14 us

profile of v4, /device:TPU:72, one launch (start us, length us, event | category | flops | bytes accessed | tf_op | source)
XLA Modules:
  0.0 66.3 jit_solution(1437111007515031193)
XLA Ops:
  0.6 62.5 %shard_map.30 = (f32[8,1,128]{2,1,0:T(1,128)}, f32[1024,128]{1,0:T(8,128)}) custom-call(bf16[1024,128]{1,0:T(8,128)(2,1)} %pts.1), custom_call_target="tpu_custom_call" | custom-call | tf_op jit(solution)/shard_map/pallas_call | solution.py:381
  63.2 0.0 copy-start
  63.2 0.7 %copy-done = f32[8,1,128]{2,1,0:T(1,128)S(1)} copy-done((f32[8,1,128]{2,1,0:T(1,128)S(1)}, f32[8,1,128]{2,1,0:T(1,128)}, u32[]{:S(2)}) %copy-start) | copy-done | bytes 4120
  63.9 0.6 copy.5
  64.5 1.9 %copy.6 = f32[1024,128]{1,0:T(8,128)} copy(f32[1024,128]{1,0:T(8,128)} %get-tuple-element.9) | data formatting | bytes 1048576
Async XLA Ops:
  63.2 0.7 %copy-start = (f32[8,1,128]{2,1,0:T(1,128)S(1)}, f32[8,1,128]{2,1,0:T(1,128)}, u32[]{:S(2)}) copy-start(f32[8,1,128]{2,1,0:T(1,128)} %get-tuple-element.4) | copy-start | bytes 12292

commit v5 on v4

--- a/solution.py
+++ b/solution.py
@@ -13,6 +13,22 @@
 LEAD = 2
 MESH = pl.DeviceIdType.MESH
 LOG2E = math.log2(math.e)
+
+
+SCALE = 8192.0
+
+
+def encode(value):
+    power = value * SCALE
+    for _ in range(3):
+        power = power * power
+    return jnp.where(value < 0.0, -power, power).astype(jnp.bfloat16)
+
+
+def decode(code):
+    power = code.astype(jnp.float32)
+    size = jnp.sqrt(jnp.sqrt(jnp.sqrt(jnp.abs(power)))) * (1.0 / SCALE)
+    return jnp.where(power < 0.0, -size, size)
 
 
 def split3(value):
@@ -48,7 +64,7 @@
     out_numer, out_two, sib_numer, sib_two,
     numer, sum_two, far_numer, far_two, got_numer, got_two, disp_mine, pot_all,
     send_sem, local_sem, rv_mate, rv_pts, rv_one, rv_snum, rv_stwo,
-    rv_xnum, rv_xtwo, rv_num, rv_two, rv_disp, rv_side, rv_fin,
+    rv_xnum, rv_xtwo, rv_num, rv_two, rv_disp, rv_fin,
 ):
     rows = pts.shape[0]
     blocks = rows // LANES
@@ -326,7 +342,7 @@
     weighted = got_numer[0]
     for q in range(1, depth):
         weighted = weighted + got_numer[q]
-    disp_mine[...] = pts[part_at(r), :].astype(jnp.float32) - weighted / divisor
+    disp_mine[...] = encode(pts[part_at(r), :].astype(jnp.float32) - weighted / divisor)
 
     def disp_copy(owner, target):
         return remote(
@@ -334,36 +350,26 @@
             send_sem.at[10], rv_disp.at[owner], {"rep": target},
         )
 
-    def side_copy(owner, src, target):
-        return remote(
-            src, disp_out.at[part_at(owner), :],
-            send_sem.at[11], rv_side.at[owner], {"rep": target},
-        )
-
-    opposite = lax.rem(z_peer(depth // 2) + depth, reps)
-    side_copy(r, disp_mine, opposite).start()
-    side_copy(r, disp_mine, across).start()
-    each(1, depth, lambda k: disp_copy(r, z_peer(k)).start())
-    pend.append(lambda: each(1, depth, lambda k: disp_copy(r, r).wait_send()))
-    pend.append(lambda: each(0, depth, lambda k: side_copy(r, disp_mine, across).wait_send()))
+    def by_distance(j):
+        k = j // 2 + 1
+        return k + lax.rem(j, 2) * (depth - 2 * k)
+
+    def send_disp(j):
+        q = z_peer(by_distance(depth - 2 - j))
+        disp_copy(r, lax.rem(q + depth, reps)).start()
+        disp_copy(r, q).start()
+
+    each(0, depth - 1, send_disp)
+    disp_copy(r, across).start()
+    pend.append(lambda: each(1, reps, lambda k: disp_copy(r, r).wait_send()))
     keep = pltpu.make_async_copy(disp_mine, disp_out.at[part_at(r), :], local_sem)
     keep.start()
-
-    def pass_on(k):
-        q = z_peer(k)
-        disp_copy(q, r).wait_recv()
-
-        @pl.when(k != depth // 2)
-        def _():
-            side_copy(q, disp_out.at[part_at(q), :], across).start()
-
-    each(1, depth, pass_on)
     each(1, reps, lambda k: fin_copy(rep_peer(k), r).wait_recv())
     low_lane = lax.broadcasted_iota(jnp.int32, (1, LANES), 1) < PART
     for b in range(blocks):
         pot_out[b] = jnp.where(low_lane, pot_all[2 * b], pot_all[2 * b + 1])
     finish()
-    each(0, depth, lambda k: side_copy(lax.rem(z_peer(k) + depth, reps), disp_mine, r).wait_recv())
+    each(1, reps, lambda k: disp_copy(rep_peer(k), r).wait_recv())
     keep.wait()
 
 
@@ -378,11 +384,11 @@
     f32 = jnp.float32
     dma = pltpu.SemaphoreType.DMA
     vmem = pltpu.VMEM
-    potential, displacement = pl.pallas_call(
+    potential, code = pl.pallas_call(
         functools.partial(body, teams, reps),
         out_shape=(
             jax.ShapeDtypeStruct((blocks, 1, LANES), f32),
-            jax.ShapeDtypeStruct((rows, width), f32),
+            jax.ShapeDtypeStruct((rows, width), jnp.bfloat16),
         ),
         in_specs=[pl.BlockSpec(memory_space=pltpu.VMEM)],
         out_specs=(
@@ -408,7 +414,7 @@
             vmem((blocks // 2, 1, LANES), f32),
             vmem((depth, PART, width), f32),
             vmem((depth, 1, LANES), f32),
-            vmem((PART, width), f32),
+            vmem((PART, width), jnp.bfloat16),
             vmem((reps, 1, LANES), f32),
             dma((12,)),
             dma,
@@ -423,11 +429,10 @@
             dma((depth,)),
             dma((reps,)),
             dma((reps,)),
-            dma((reps,)),
         ],
         compiler_params=pltpu.CompilerParams(collective_id=0, has_side_effects=True),
     )(points)
-    return potential.reshape(rows), displacement
+    return potential.reshape(rows), decode(code)
 
 
 def solution(mesh):

time: 66.6 us -> 59.4 us (0.89)
  the two profiles are of different devices: /device:TPU:72 before, /device:TPU:1 now
where the time goes in v5:
time: 59.4 us; the launch traced here: 58.7 us
  Pallas kernels  55.2 us (93%)
  other arithmetic  2.21 us (4%)
  between operations  0.65 us (1%)
  local copies, waits for them, and re-layouts  0.6 us (1%)
    pallas_call x1, Pallas kernels, shards(): pl.pallas_call(functools.partial(body, teams, reps), out_shape=(jax.Shape...  55.2 us
    select_n x1, other arithmetic, decode(): return jnp.where(power < 0.0, -size, size)  2.21 us

profile of v5, /device:TPU:1, one launch (start us, length us, event | category | flops | bytes accessed | tf_op | source)
XLA Modules:
  0.0 58.7 jit_solution(14210390127403487351)
XLA Ops:
  0.6 55.2 %shard_map.30 = (f32[8,1,128]{2,1,0:T(1,128)}, bf16[1024,128]{1,0:T(8,128)(2,1)}) custom-call(bf16[1024,128]{1,0:T(8,128)(2,1)} %pts.1), custom_call_target="tpu_custom_call" | custom-call | tf_op jit(solution)/shard_map/pallas_call | solution.py:387
  55.8 0.0 copy-start
  55.9 2.2 %negate_select_fusion = f32[1024,128]{1,0:T(8,128)} fusion(bf16[1024,128]{1,0:T(8,128)(2,1)} %get-tuple-element.5), kind=kLoop, calls=%fused_computation | loop fusion | flops 786432 | bytes 786432 | tf_op jit(solution)/shard_map/jit(_where)/select_n | solution.py:31
  58.1 0.0 copy-done
  58.1 0.6 %copy.4 = f32[1024]{0:T(1024)} copy(f32[1024]{0:T(1024)S(1)} %bitcast.1) | data formatting | bytes 8192
Async XLA Ops:
  55.8 2.2 %copy-start = (f32[8,1,128]{2,1,0:T(1,128)S(1)}, f32[8,1,128]{2,1,0:T(1,128)}, u32[]{:S(2)}) copy-start(f32[8,1,128]{2,1,0:T(1,128)} %get-tuple-element.4) | copy-start | bytes 12292

commit v6 on v5

--- a/solution.py
+++ b/solution.py
@@ -27,7 +27,7 @@
 
 def decode(code):
     power = code.astype(jnp.float32)
-    size = jnp.sqrt(jnp.sqrt(jnp.sqrt(jnp.abs(power)))) * (1.0 / SCALE)
+    size = jnp.exp2(jnp.log2(jnp.abs(power)) * 0.125) * (1.0 / SCALE)
     return jnp.where(power < 0.0, -size, size)
 
 
@@ -58,13 +58,19 @@
     return jnp.sum(jnp.where(lane == sub, total, 0.0), axis=0, keepdims=True)
 
 
+def column_of(row, size, first):
+    lane = lax.broadcasted_iota(jnp.int32, (size, LANES), 1)
+    sub = lax.broadcasted_iota(jnp.int32, (size, LANES), 0)
+    return jnp.sum(jnp.where(lane == sub + first, row, 0.0), axis=1, keepdims=True)
+
+
 def body(
     teams, reps, pts, pot_out, disp_out,
-    mate, rows_aug, cols, expo, chip_one, got_one, pot, pot_scaled,
+    mate, rows_aug, cols, first_exp, chip_one, got_one, pot, weight,
     out_numer, out_two, sib_numer, sib_two,
-    numer, sum_two, far_numer, far_two, got_numer, got_two, disp_mine, pot_all,
+    numer, sum_two, got_numer, got_two, disp_mine, pot_all,
     send_sem, local_sem, rv_mate, rv_pts, rv_one, rv_snum, rv_stwo,
-    rv_xnum, rv_xtwo, rv_num, rv_two, rv_disp, rv_fin,
+    rv_num, rv_two, rv_disp, rv_fin,
 ):
     rows = pts.shape[0]
     blocks = rows // LANES
@@ -183,9 +189,9 @@
             tile = lax.dot_general(
                 rows_aug[pl.ds(b * 256, 256), :], wide, nt, preferred_element_type=jnp.float32
             )
-            tile = tile * (0.5 * LOG2E)
-            expo[c, pl.ds(b * 256, 256), :] = tile
-            acc = acc + jnp.sum(jnp.exp2(0.5 * tile), axis=0, keepdims=True)
+            tile = jnp.exp2(tile * (0.25 * LOG2E))
+            first_exp[c, pl.ds(b * 256, 256), :] = tile
+            acc = acc + jnp.sum(tile, axis=0, keepdims=True)
         chip_one[pl.ds(c, 1), :] = acc
         return carry
 
@@ -205,14 +211,16 @@
         first = first + got_one[q]
     pot[...] = -2.0 * (jnp.log(first) - log_count)
 
-    pot_scaled[...] = pot[...] * (0.5 * LOG2E)
+    weight[...] = jnp.exp2(pot[...] * (0.5 * LOG2E))
 
     def second_block(b):
         acc = jnp.zeros((LANES, LANES), jnp.float32)
         total = jnp.zeros((LANES, LANES), jnp.float32)
         for s in range(chunks // 2):
-            left = jnp.exp2(expo[2 * s, block_at(b), :] + pot_scaled[2 * s : 2 * s + 1, :])
-            right = jnp.exp2(expo[2 * s + 1, block_at(b), :] + pot_scaled[2 * s + 1 : 2 * s + 2, :])
+            left = first_exp[2 * s, block_at(b), :]
+            left = left * weight[2 * s : 2 * s + 1, :] * left
+            right = first_exp[2 * s + 1, block_at(b), :]
+            right = right * weight[2 * s + 1 : 2 * s + 2, :] * right
             acc = acc + left + right
             rounded = jnp.concatenate(
                 [left.astype(jnp.bfloat16), right.astype(jnp.bfloat16)], axis=1
@@ -232,20 +240,8 @@
             out_two.at[b], sib_two.at[b], send_sem.at[4], rv_stwo.at[b], {"team": sibling}
         )
 
-    def xnum_copy(b, slot):
-        return remote(
-            numer.at[block_at(b), :], far_numer.at[slot],
-            send_sem.at[5], rv_xnum.at[slot], {"rep": across},
-        )
-
-    def xtwo_copy(b, slot):
-        return remote(
-            sum_two.at[b], far_two.at[slot],
-            send_sem.at[6], rv_xtwo.at[slot], {"rep": across},
-        )
-
     def turn(i):
-        return lax.rem(z // 2 + 1 + i, half_blocks)
+        return lax.rem(z // 2 + 2 - i + (i // 2) * (7 - 2 * i) + half_blocks, half_blocks)
 
     def num_copy(dest, owner):
         return remote(
@@ -260,11 +256,10 @@
         )
 
     def place(i):
-        side, slot = i // half_blocks, turn(lax.rem(i, half_blocks))
-        return side, slot, lax.rem(1 - near + side, 2) * half_blocks + slot
+        return lax.rem(1 - near + i, 2) * half_blocks + turn(i // 2)
 
     def for_sibling(i):
-        b = place(i)[2]
+        b = place(i)
         row, total = second_block(blocks + b)
         out_numer[b] = total
         out_two[b] = row
@@ -272,31 +267,21 @@
         stwo_copy(b).start()
 
     def for_own(i):
-        side, slot, b = place(i)
+        b = place(i)
         row, total = second_block(b)
         snum_copy(b).wait_recv()
         stwo_copy(b).wait_recv()
-        numer[block_at(b), :] = total + sib_numer[b]
-        sum_two[b] = row + sib_two[b]
-
-        @pl.when(side == 0)
-        def _():
-            xnum_copy(b, slot).start()
-            xtwo_copy(b, slot).start()
-
-        @pl.when(side == 1)
-        def _():
-            xnum_copy(b, slot).wait_recv()
-            xtwo_copy(b, slot).wait_recv()
-            numer[block_at(b), :] = numer[block_at(b), :] + far_numer[slot]
-            sum_two[b] = sum_two[b] + far_two[slot]
-            for h in range(2):
-                q = 2 * b + h
-
-                @pl.when(q != r)
-                def _():
-                    two_copy(b, q, z).start()
-                    num_copy(q, z).start()
+        row = row + sib_two[b]
+        sum_two[b] = row
+        mean = (total + sib_numer[b]) / jnp.maximum(column_of(row, LANES, 0), 1e-30)
+        numer[block_at(b), :] = encode(pts[block_at(b), :].astype(jnp.float32) - mean)
+        for h in range(2):
+            q = 2 * b + h
+
+            @pl.when(q != r)
+            def _():
+                two_copy(b, q, r).start()
+                num_copy(q, r).start()
 
     def second_step(i, carry):
         @pl.when(i < blocks)
@@ -312,15 +297,13 @@
     lax.fori_loop(0, blocks + LEAD, second_step, 0)
     pend.append(lambda: each(0, blocks, lambda k: snum_copy(k).wait_send()))
     pend.append(lambda: each(0, blocks, lambda k: stwo_copy(k).wait_send()))
-    pend.append(lambda: each(0, half_blocks, lambda k: xnum_copy(k, k).wait_send()))
-    pend.append(lambda: each(0, half_blocks, lambda k: xtwo_copy(k, k).wait_send()))
-    pend.append(lambda: each(1, depth, lambda k: num_copy(r, z).wait_send()))
-    pend.append(lambda: each(1, depth, lambda k: two_copy(0, r, z).wait_send()))
-    got_two[z] = sum_two[r // 2]
-    got_numer[z] = numer[part_at(r), :]
-    each(1, depth, lambda k: two_copy(0, r, lax.rem(z + k, depth)).wait_recv())
+    pend.append(lambda: each(1, reps, lambda k: num_copy(r, r).wait_send()))
+    pend.append(lambda: each(1, reps, lambda k: two_copy(0, r, r).wait_send()))
+    got_two[r] = sum_two[r // 2]
+    got_numer[r] = numer[part_at(r), :]
+    each(1, reps, lambda k: two_copy(0, r, rep_peer(k)).wait_recv())
     second = got_two[0]
-    for q in range(1, depth):
+    for q in range(1, reps):
         second = second + got_two[q]
     half = lax.rem(r, 2)
     pot_own = pot[pl.ds(home, 1), :]
@@ -335,14 +318,13 @@
 
     each(1, reps, lambda k: fin_copy(r, rep_peer(k)).start())
     pend.append(lambda: each(1, reps, lambda k: fin_copy(r, r).wait_send()))
-    lane = lax.broadcasted_iota(jnp.int32, (PART, LANES), 1)
-    sub = lax.broadcasted_iota(jnp.int32, (PART, LANES), 0)
-    divisor = jnp.sum(jnp.where(lane == sub + half * PART, second, 0.0), axis=1, keepdims=True)
-    each(1, depth, lambda k: num_copy(r, lax.rem(z + k, depth)).wait_recv())
-    weighted = got_numer[0]
-    for q in range(1, depth):
-        weighted = weighted + got_numer[q]
-    disp_mine[...] = encode(pts[part_at(r), :].astype(jnp.float32) - weighted / divisor)
+    divisor = column_of(second, PART, half * PART)
+    shares = [column_of(got_two[q], PART, half * PART) / divisor for q in range(reps)]
+    each(1, reps, lambda k: num_copy(r, rep_peer(k)).wait_recv())
+    moved = decode(got_numer[0]) * shares[0]
+    for q in range(1, reps):
+        moved = moved + decode(got_numer[q]) * shares[q]
+    disp_mine[...] = encode(moved)
 
     def disp_copy(owner, target):
         return remote(
@@ -367,7 +349,7 @@
     each(1, reps, lambda k: fin_copy(rep_peer(k), r).wait_recv())
     low_lane = lax.broadcasted_iota(jnp.int32, (1, LANES), 1) < PART
     for b in range(blocks):
-        pot_out[b] = jnp.where(low_lane, pot_all[2 * b], pot_all[2 * b + 1])
+        pot_out[pl.ds(b, 1), :] = jnp.where(low_lane, pot_all[2 * b], pot_all[2 * b + 1])
     finish()
     each(1, reps, lambda k: disp_copy(rep_peer(k), r).wait_recv())
     keep.wait()
@@ -387,7 +369,7 @@
     potential, code = pl.pallas_call(
         functools.partial(body, teams, reps),
         out_shape=(
-            jax.ShapeDtypeStruct((blocks, 1, LANES), f32),
+            jax.ShapeDtypeStruct((blocks, LANES), f32),
             jax.ShapeDtypeStruct((rows, width), jnp.bfloat16),
         ),
         in_specs=[pl.BlockSpec(memory_space=pltpu.VMEM)],
@@ -408,12 +390,10 @@
             vmem((blocks, 1, LANES), f32),
             vmem((blocks, LANES, width), f32),
             vmem((blocks, 1, LANES), f32),
-            vmem((rows, width), f32),
+            vmem((rows, width), jnp.bfloat16),
             vmem((blocks, 1, LANES), f32),
-            vmem((blocks // 2, LANES, width), f32),
-            vmem((blocks // 2, 1, LANES), f32),
-            vmem((depth, PART, width), f32),
-            vmem((depth, 1, LANES), f32),
+            vmem((reps, PART, width), jnp.bfloat16),
+            vmem((reps, 1, LANES), f32),
             vmem((PART, width), jnp.bfloat16),
             vmem((reps, 1, LANES), f32),
             dma((12,)),
@@ -423,10 +403,8 @@
             dma((chips,)),
             dma((blocks,)),
             dma((blocks,)),
-            dma((blocks // 2,)),
-            dma((blocks // 2,)),
-            dma((depth,)),
-            dma((depth,)),
+            dma((reps,)),
+            dma((reps,)),
             dma((reps,)),
             dma((reps,)),
         ],

time: 59.4 us -> 57.5 us (0.968)
  Pallas kernels: 55.2 us -> 54.1 us
    pallas_call x1, Pallas kernels: 55.2 us -> 54.1 us  [shards(): pl.pallas_call(functools.partial(body, teams, reps), out_shape=(jax.Shape...]
where the time goes in v6:
time: 57.5 us; the launch traced here: 57.3 us
  Pallas kernels  54.1 us (94%)
  other arithmetic  1.94 us (3%)
  between operations  0.65 us (1%)
  local copies, waits for them, and re-layouts  0.6 us (1%)
    pallas_call x1, Pallas kernels, shards(): pl.pallas_call(functools.partial(body, teams, reps), out_shape=(jax.Shape...  54.1 us
    select_n x1, other arithmetic, decode(): return jnp.where(power < 0.0, -size, size)  1.94 us

profile of v6, /device:TPU:1, one launch (start us, length us, event | category | flops | bytes accessed | tf_op | source)
XLA Modules:
  0.0 57.3 jit_solution(13978480223846172603)
XLA Ops:
  0.6 54.1 %shard_map.30 = (f32[8,128]{1,0:T(8,128)}, bf16[1024,128]{1,0:T(8,128)(2,1)}) custom-call(bf16[1024,128]{1,0:T(8,128)(2,1)} %pts.1), custom_call_target="tpu_custom_call" | custom-call | tf_op jit(solution)/shard_map/pallas_call | solution.py:369
  54.8 0.0 copy-start
  54.8 1.9 %negate_select_fusion = f32[1024,128]{1,0:T(8,128)} fusion(bf16[1024,128]{1,0:T(8,128)(2,1)} %get-tuple-element.5), kind=kLoop, calls=%fused_computation | loop fusion | flops 917504 | bytes 786432 | tf_op jit(solution)/shard_map/jit(_where)/select_n | solution.py:31
  56.7 0.0 copy-done
  56.7 0.6 %copy.4 = f32[1024]{0:T(1024)} copy(f32[1024]{0:T(1024)S(1)} %bitcast.1) | data formatting | bytes 8192
Async XLA Ops:
  54.8 2.0 %copy-start = (f32[8,128]{1,0:T(8,128)S(1)}, f32[8,128]{1,0:T(8,128)}, u32[]{:S(2)}) copy-start(f32[8,128]{1,0:T(8,128)} %get-tuple-element.4) | copy-start | bytes 12292

commit v7 on v6

--- a/solution.py
+++ b/solution.py
@@ -65,7 +65,8 @@
 
 
 def body(
-    teams, reps, pts, pot_out, disp_out,
+    teams, reps, source, pot_out, disp_out,
+    pts,
     mate, rows_aug, cols, first_exp, chip_one, got_one, pot, weight,
     out_numer, out_two, sib_numer, sib_two,
     numer, sum_two, got_numer, got_two, disp_mine, pot_all,
@@ -133,13 +134,17 @@
     each(1, chips, lambda k: greet({"team": same_core(k)}))
     greet({"team": sibling})
     each(1, reps, lambda k: greet({"rep": rep_peer(k)}))
-    own = pltpu.make_async_copy(pts.at[part_at(r), :], cols.at[part_at(t // 2), :], local_sem)
+    own = pltpu.make_async_copy(
+        source.at[part_at(r), :], cols.at[part_at(t // 2), :], local_sem.at[0]
+    )
     own.start()
+    load = pltpu.make_async_copy(source, pts, local_sem.at[1])
+    load.start()
     pl.semaphore_wait(barrier, chips + reps - 1)
 
     def points_copy(owner, target):
         return remote(
-            pts.at[part_at(r), :], cols.at[part_at(owner), :],
+            source.at[part_at(r), :], cols.at[part_at(owner), :],
             send_sem.at[0], rv_pts.at[owner], {"team": target},
         )
 
@@ -155,10 +160,11 @@
 
     lax.fori_loop(0, chunks, send_points, 0)
     pend.append(lambda: each(1, chips, lambda k: points_copy(t // 2, t).wait_send()))
-    mate_copy = remote(pts, mate, send_sem.at[1], rv_mate, {"team": sibling})
+    mate_copy = remote(source, mate, send_sem.at[1], rv_mate, {"team": sibling})
     mate_copy.start()
     pend.append(mate_copy.wait_send)
     own.wait()
+    load.wait()
 
     def widen_from(ref, first):
         def widen_rows(b, carry):
@@ -344,7 +350,7 @@
     each(0, depth - 1, send_disp)
     disp_copy(r, across).start()
     pend.append(lambda: each(1, reps, lambda k: disp_copy(r, r).wait_send()))
-    keep = pltpu.make_async_copy(disp_mine, disp_out.at[part_at(r), :], local_sem)
+    keep = pltpu.make_async_copy(disp_mine, disp_out.at[part_at(r), :], local_sem.at[0])
     keep.start()
     each(1, reps, lambda k: fin_copy(rep_peer(k), r).wait_recv())
     low_lane = lax.broadcasted_iota(jnp.int32, (1, LANES), 1) < PART
@@ -353,6 +359,11 @@
     finish()
     each(1, reps, lambda k: disp_copy(rep_peer(k), r).wait_recv())
     keep.wait()
+
+
+def finish_body(pot, code, pot_out, disp_out):
+    pot_out[...] = pot[...]
+    disp_out[...] = decode(code[...])
 
 
 def shards(points):
@@ -372,12 +383,13 @@
             jax.ShapeDtypeStruct((blocks, LANES), f32),
             jax.ShapeDtypeStruct((rows, width), jnp.bfloat16),
         ),
-        in_specs=[pl.BlockSpec(memory_space=pltpu.VMEM)],
+        in_specs=[pl.BlockSpec(memory_space=pl.ANY)],
         out_specs=(
             pl.BlockSpec(memory_space=pltpu.VMEM),
             pl.BlockSpec(memory_space=pl.ANY),
         ),
         scratch_shapes=[
+            vmem((rows, width), jnp.bfloat16),
             vmem((rows, width), jnp.bfloat16),
             vmem((2 * rows, 2 * width), jnp.bfloat16),
             vmem((chips * PART, width), jnp.bfloat16),
@@ -397,7 +409,7 @@
             vmem((PART, width), jnp.bfloat16),
             vmem((reps, 1, LANES), f32),
             dma((12,)),
-            dma,
+            dma((2,)),
             dma,
             dma((chips,)),
             dma((chips,)),
@@ -410,7 +422,23 @@
         ],
         compiler_params=pltpu.CompilerParams(collective_id=0, has_side_effects=True),
     )(points)
-    return potential.reshape(rows), decode(code)
+    potential, displacement = pl.pallas_call(
+        finish_body,
+        grid=(2,),
+        out_shape=(
+            jax.ShapeDtypeStruct((blocks, LANES), f32),
+            jax.ShapeDtypeStruct((rows, width), f32),
+        ),
+        in_specs=[
+            pl.BlockSpec((blocks, LANES), lambda i: (0, 0)),
+            pl.BlockSpec((rows // 2, width), lambda i: (i, 0)),
+        ],
+        out_specs=(
+            pl.BlockSpec((blocks, LANES), lambda i: (0, 0)),
+            pl.BlockSpec((rows // 2, width), lambda i: (i, 0)),
+        ),
+    )(potential, code)
+    return potential.reshape(rows), displacement
 
 
 def solution(mesh):

time: 57.5 us -> 56.3 us (0.979)
  other arithmetic: 1.94 us -> 0 us
  Pallas kernels: 54.1 us -> 55.5 us
  local copies, waits for them, and re-layouts: 0.6 us -> 0 us
    select_n x1 -> x0, other arithmetic: 1.94 us -> none  [decode(): return jnp.where(power < 0.0, -size, size)]
    pallas_call x0 -> x1, Pallas kernels: none -> 1.81 us  [shards(): pl.pallas_call(finish_body, grid=(2,), out_shape=(jax.ShapeDtypeStruct((b...]
    unnamed x3 -> x0, local copies, waits for them, and re-layouts: 0.6 us -> none
where the time goes in v7:
time: 56.3 us; the launch traced here: 56.2 us
  Pallas kernels  55.5 us (99%)
  between operations  0.64 us (1%)
    pallas_call x1, Pallas kernels, shards(): pl.pallas_call(functools.partial(body, teams, reps), out_shape=(jax.Shape...  53.7 us
    pallas_call x1, Pallas kernels, shards(): pl.pallas_call(finish_body, grid=(2,), out_shape=(jax.ShapeDtypeStruct((b...  1.81 us

profile of v7, /device:TPU:1, one launch (start us, length us, event | category | flops | bytes accessed | tf_op | source)
XLA Modules:
  0.0 56.2 jit_solution(16065309868384467421)
XLA Ops:
  0.6 53.7 %shard_map.30 = (f32[8,128]{1,0:T(8,128)}, bf16[1024,128]{1,0:T(8,128)(2,1)}) custom-call(bf16[1024,128]{1,0:T(8,128)(2,1)} %source.1), custom_call_target="tpu_custom_call" | custom-call | tf_op jit(solution)/shard_map/pallas_call | solution.py:380
  54.3 1.8 %shard_map.31 = (f32[8,128]{1,0:T(8,128)}, f32[1024,128]{1,0:T(8,128)}) custom-call(f32[8,128]{1,0:T(8,128)} %get-tuple-element.6.pot, bf16[1024,128]{1,0:T(8,128)(2,1)} %get-tuple-element.7.code), custom_call_target="tpu_custom_call" | custom-call | tf_op jit(solution)/shard_map/pallas_call | solution.py:425
